TPU v7x, 32 devices: a whole 2x2x4 slice. The times are simulated.
32 devices in a mesh: groups: 2 (over y), psg: 16 (over z, x, core).
Axes of the slice: x: 2, y: 2, z: 4, core: 2. Of those that a mesh axis runs over, the one named last changes fastest.
Arguments:
- tail_hidden_states: bfloat16 [256, 8192], P('groups', 'psg'), parts along dimension 0, may hold values from -6 to 6
- passage_hidden_states: bfloat16 [2048, 8192], P(('groups', 'psg')), parts along dimension 0, may hold values from -6 to 6
- lengths: int32 [4], P('groups'), parts along dimension 0, may hold values from 1 to 768, 1024 in all
- storage_order: int32 [4], P('groups'), parts along dimension 0, may hold values from 0 to 1, each once
- orders: int32 [6, 2], P('groups'), parts along dimension 0, may hold values from 0 to 1, each once within a row
- w_query: bfloat16 [8192, 4096], P('psg'), may hold values from -1 to 1
- key_weight: bfloat16 [8192, 512], P('psg'), may hold values from -0.0625 to 0.0625
- value_weight: bfloat16 [8192, 512], P('psg'), may hold values from -0.0625 to 0.0625
- w_out: bfloat16 [4096, 8192], P(None, 'psg'), may hold values from -0.09375 to 0.09375
- norm_gain: float32 [8192], P('psg'), may hold values from 0.1 to 1.9
Outputs:
- layer_out: bfloat16 [256, 8192], P('groups', 'psg'), parts along dimension 0
There are 2 independent parts, one for each index of `groups`. A program takes and returns all parts, laid end to end along the dimension named above; an argument that names none is the same for every part. Nothing has to cross between parts.
Inputs may be any that keep to these rules, and one draw needn't show every extreme that they name: `lengths`: they sum to 1024; the largest is 768. `storage_order`: A permutation of the passages. `orders`: each row is a permutation of the passages.
All inputs are finite; a program needn't handle non-finite values.
Results may differ from a plain program's by a relative error of at most 0.01065.
The roundings to bfloat16 on the way count: a program that leaves them out, or rounds other values in their place, can miss the bound.
Values may be sent and summed in bfloat16 or wider, within the bound.
No kernel may reach another device: no remote copies, remote signals or barrier semaphores. Data moves between devices by JAX's collectives and lax.ppermute only.
A program may use at most 128 MiB of HBM per device.

v0:
```python
import functools

import jax
import jax.numpy as jnp
import numpy as np
from jax import lax
from jax.experimental import pallas as pl
from jax.experimental.pallas import tpu as pltpu
from jax.sharding import PartitionSpec as P


MODEL_WIDTH = 8192
HEAD_SIZE = 128


theta_base = 500000.0
epsilon = 1e-05


def joined(part, axis, combine):
    gathered = jax.tree.map(lambda a: lax.all_gather(a, axis), part)

    def take(source):
        return jax.tree.map(lambda a: lax.dynamic_index_in_dim(a, source, 0, False), gathered)

    return lax.fori_loop(
        1, lax.axis_size(axis), lambda source, state: combine(state, take(source)), take(0)
    )


def rotate(vectors, places):
    half = vectors.shape[-1] // 2
    freqs = theta_base ** (-jnp.arange(half, dtype=jnp.float32) * 2.0 / vectors.shape[-1])
    angles = places.astype(jnp.float32)[:, None] * freqs[None, :]
    cosine = jnp.cos(angles)[:, None, :]
    sine = jnp.sin(angles)[:, None, :]
    first = vectors[..., :half]
    second = vectors[..., half:]
    return jnp.concatenate(
        [first * cosine - second * sine, second * cosine + first * sine], axis=-1
    )


def general_device(
    tail_hidden_states,
    passage_hidden_states,
    lengths,
    storage_order,
    orders,
    w_query,
    key_weight,
    value_weight,
    w_out,
    norm_gain,
):
    shards = lax.axis_size("psg")
    device = lax.axis_index("psg")
    row_count = passage_hidden_states.shape[0]
    tail_count = tail_hidden_states.shape[0]
    kv_heads = key_weight.shape[1] // HEAD_SIZE
    query_heads = w_query.shape[1] // HEAD_SIZE
    query_group = query_heads // kv_heads
    total_keys = row_count * shards
    query_part = jnp.dot(tail_hidden_states, w_query, preferred_element_type=jnp.float32)
    key_part = jnp.dot(tail_hidden_states, key_weight, preferred_element_type=jnp.float32)
    value_part = jnp.dot(tail_hidden_states, value_weight, preferred_element_type=jnp.float32)
    query_sum, key_sum, value_sum = lax.psum((query_part, key_part, value_part), "psg")
    tail_pos = total_keys + jnp.arange(tail_count, dtype=jnp.int32)
    query_vectors = rotate(query_sum.reshape(tail_count, query_heads, HEAD_SIZE), tail_pos).astype(
        jnp.bfloat16
    )
    query_vectors = query_vectors.reshape(tail_count, kv_heads, query_group, HEAD_SIZE)
    tail_key_rows = rotate(key_sum.reshape(tail_count, kv_heads, HEAD_SIZE), tail_pos).astype(
        jnp.bfloat16
    )
    tail_value_rows = value_sum.astype(jnp.bfloat16).reshape(tail_count, kv_heads, HEAD_SIZE)

    def add_block(piece):
        return jnp.dot(passage_hidden_states, piece, preferred_element_type=jnp.float32)

    unrotated_key = add_block(lax.all_gather(key_weight, "psg", axis=0, tiled=True))
    raw_value = add_block(lax.all_gather(value_weight, "psg", axis=0, tiled=True))
    numbers = jnp.arange(lengths.shape[0], dtype=jnp.int32)
    pick = (storage_order[:, None] == numbers[None, :]).astype(jnp.int32)
    stored_lengths = jnp.sum(pick * lengths[None, :], axis=1)
    ends = jnp.cumsum(stored_lengths)
    starts = ends - stored_lengths
    row_ids = device * row_count + jnp.arange(row_count, dtype=jnp.int32)
    slots = jnp.sum((ends[None, :] <= row_ids[:, None]).astype(jnp.int32), axis=1)
    in_slot = (slots[:, None] == numbers[None, :]).astype(jnp.int32)
    offsets = row_ids - jnp.sum(in_slot * starts[None, :], axis=1)
    passage_hot = jnp.dot(in_slot, pick)
    ordered_hot = (orders[:, :, None] == numbers[None, None, :]).astype(jnp.int32)
    ordered_lengths = jnp.sum(ordered_hot * lengths[None, None, :], axis=2)
    order_starts = jnp.cumsum(ordered_lengths, axis=1) - ordered_lengths
    placed = jnp.sum(ordered_hot * order_starts[:, :, None], axis=1)
    token_positions = (
        jnp.sum(passage_hot[None, :, :] * placed[:, None, :], axis=2) + offsets[None, :]
    )
    passage_values = raw_value.astype(jnp.bfloat16).reshape(row_count, kv_heads, HEAD_SIZE)
    unrotated_key = unrotated_key.reshape(row_count, kv_heads, HEAD_SIZE)
    scale = HEAD_SIZE ** (-0.5)
    tail_scores = (
        jnp.einsum(
            "tkgd,skd->tkgs", query_vectors, tail_key_rows, preferred_element_type=jnp.float32
        )
        * scale
    )
    causal = jnp.arange(tail_count)[None, :] <= jnp.arange(tail_count)[:, None]
    tail_scores = jnp.where(causal[:, None, None, :], tail_scores, -1e30)
    tail_top = jnp.max(tail_scores, axis=-1)

    def scores_for(places):
        keys = rotate(unrotated_key, places).astype(jnp.bfloat16)
        return (
            jnp.einsum("tkgd,nkd->tkgn", query_vectors, keys, preferred_element_type=jnp.float32)
            * scale
        )

    def local_stats(places):
        scores = scores_for(places)
        peak = jnp.maximum(jnp.max(scores, axis=-1), tail_top)
        return (peak, jnp.sum(jnp.exp(scores - peak[..., None]), axis=-1))

    def combine(first, second):
        peak = jnp.maximum(first[0], second[0])
        return (peak, first[1] * jnp.exp(first[0] - peak) + second[1] * jnp.exp(second[0] - peak))

    peaks, totals = joined(lax.map(local_stats, token_positions), "psg", combine)

    def accumulate(running, inputs):
        places, peak, partial_value = inputs
        weights = jnp.exp(scores_for(places) - peak[..., None])
        tail_weights = jnp.exp(tail_scores - peak[..., None])
        denom = (partial_value + jnp.sum(tail_weights, axis=-1))[..., None]
        shared = jnp.einsum(
            "tkgn,nkd->tkgd",
            weights.astype(jnp.bfloat16),
            passage_values,
            preferred_element_type=jnp.float32,
        )
        own = jnp.einsum(
            "tkgs,skd->tkgd",
            tail_weights.astype(jnp.bfloat16),
            tail_value_rows,
            preferred_element_type=jnp.float32,
        )
        return ((running[0] + shared / denom, running[1] + own / denom), None)

    start_sums = jnp.zeros((tail_count, kv_heads, query_group, HEAD_SIZE), jnp.float32)
    (shared_sum, own_sum), unused_slot = lax.scan(
        accumulate, (start_sums, start_sums), (token_positions, peaks, totals)
    )
    agreed_output = lax.psum(shared_sum, "psg") + own_sum
    mixed = agreed_output.reshape(tail_count, -1).astype(jnp.bfloat16)
    projected = jnp.dot(mixed, w_out, preferred_element_type=jnp.float32)
    squares = lax.psum(jnp.sum(projected * projected, axis=1), "psg")
    factor = lax.rsqrt(squares / MODEL_WIDTH + epsilon)[:, None]
    return (projected * factor * norm_gain[None, :]).astype(jnp.bfloat16)


WIRE = jnp.float16
ROWS_COLUMNS = (((1,), (1,)), ((), ()))


def granted(mebibytes):
    return pltpu.CompilerParams(vmem_limit_bytes=mebibytes << 20)


def in_vmem(count):
    return [pl.BlockSpec(memory_space=pltpu.VMEM)] * count


def table_kernel(teams, ring, rows, perms, pos, lengths, storage_order, orders, freq_ref, *out_refs):
    key_cos, key_sin, query_cos, query_sin = out_refs
    passages = lengths.shape[0]
    mine = key_cos.shape[0] - perms * teams * rows
    tokens = mine * ring
    stored = [storage_order[s] for s in range(passages)]
    starts = [jnp.int32(0)]
    for s in range(passages - 1):
        starts.append(starts[-1] + lengths[stored[s]])
    shifts = []
    for r in range(perms):
        first, placed = jnp.int32(0), [jnp.int32(0)] * passages
        for i in range(passages):
            passage = orders[r * passages + i]
            placed = [old + jnp.where(stored[s] == passage, first, 0) for s, old in enumerate(placed)]
            first = first + lengths[passage]
        shifts.append([placed[s] - starts[s] for s in range(passages)])
    lane = lax.broadcasted_iota(jnp.int32, (1, HEAD_SIZE), 1)
    sign = jnp.where(lane < HEAD_SIZE // 2, -1.0, 1.0)

    def write(cos_ref, sin_ref, first, places):
        angles = places.astype(jnp.float32) * freq_ref[...]
        place = slice(first, first + places.shape[0])
        cos_ref[place, :] = jnp.cos(angles)
        sin_ref[place, :] = jnp.sin(angles) * sign

    for ka in range(teams):
        ids = lax.broadcasted_iota(jnp.int32, (rows, HEAD_SIZE), 0) + (ka * ring + pos[1]) * rows
        for r in range(perms):
            shift = shifts[r][0]
            for s in range(1, passages):
                shift = jnp.where(ids >= starts[s], shifts[r][s], shift)
            write(key_cos, key_sin, (r * teams + ka) * rows, ids + shift)
    total = teams * ring * rows
    ids = lax.broadcasted_iota(jnp.int32, (mine, HEAD_SIZE), 0) + (total + pos[1] * mine)
    write(key_cos, key_sin, perms * teams * rows, ids)
    ids = lax.broadcasted_iota(jnp.int32, (tokens, HEAD_SIZE), 0) + total
    write(query_cos, query_sin, 0, ids)


def turned(vectors, cosine, sine):
    return vectors * cosine + pltpu.roll(vectors, HEAD_SIZE // 2, 1) * sine


def bit_order(count):
    width = count.bit_length() - 1
    return [int(format(s, "b").zfill(width)[::-1], 2) if width else 0 for s in range(count)]


def query_kernel(ring, heads, pos, x_ref, w_ref, keep_ref, send_ref, acc_ref):
    acc_ref[...] = jnp.dot(x_ref[...], w_ref[...], preferred_element_type=jnp.float32)
    tokens = x_ref.shape[0]
    for slot, kb in enumerate(bit_order(ring)):
        unit = pos[1] ^ kb
        out = keep_ref if slot < ring // 2 else send_ref
        for j in range(heads):
            column = pl.multiple_of((unit * heads + j) * HEAD_SIZE, HEAD_SIZE)
            out[slot % (ring // 2), 0, j * tokens : (j + 1) * tokens, :] = acc_ref[
                :, pl.ds(column, HEAD_SIZE)
            ]


def project(teams, ring, pos, rows_ref, w_refs, out_refs, acc_ref):
    width = w_refs[0].shape[0]
    total = None
    for kb in range(ring):
        part = jnp.dot(
            rows_ref[:, kb * width : (kb + 1) * width],
            w_refs[kb][...],
            preferred_element_type=jnp.float32,
        )
        total = part if total is None else total + part
    acc_ref[...] = total
    for ka in range(teams):
        column = pl.multiple_of((pos[0] ^ ka) * HEAD_SIZE, HEAD_SIZE)
        out_refs[ka][...] = acc_ref[:, pl.ds(column, HEAD_SIZE)].astype(out_refs[ka].dtype)


def key_kernel(teams, ring, pos, *refs):
    x_refs, t_refs, w_refs = refs[:teams], refs[teams : teams + ring], refs[teams + ring : teams + 2 * ring]
    *out_refs, all_ref, acc_ref = refs[teams + 2 * ring :]
    rows, width, mine = x_refs[0].shape[0], t_refs[0].shape[1], t_refs[0].shape[0] // ring
    for kb in range(ring):
        column = pl.multiple_of((pos[1] ^ kb) * width, width)
        place = slice(kb * width, (kb + 1) * width)
        for ka in range(teams):
            first = pl.multiple_of((pos[0] ^ ka) * rows, rows)
            all_ref[pl.ds(first, rows), place] = x_refs[ka][:, pl.ds(column, width)]
        first = pl.multiple_of(pos[1] * mine, mine)
        all_ref[teams * rows :, place] = t_refs[kb][pl.ds(first, mine), :]
    project(teams, ring, pos, all_ref, w_refs, out_refs, acc_ref)


def value_kernel(teams, ring, pos, rows_ref, *refs):
    project(teams, ring, pos, rows_ref, refs[:ring], refs[ring:-1], refs[-1])


def turn_kernel(perms, k_ref, cos_ref, sin_ref, out_ref):
    rows = (out_ref.shape[0] - k_ref.shape[0]) // (perms - 1)
    for r in range(perms):
        place = slice(r * rows, (r + 1) * rows)
        out_ref[place, :] = turned(k_ref[:rows, :], cos_ref[place, :], sin_ref[place, :]).astype(
            out_ref.dtype
        )
    out_ref[perms * rows :, :] = turned(
        k_ref[rows:, :], cos_ref[perms * rows :, :], sin_ref[perms * rows :, :]
    ).astype(out_ref.dtype)


def attend_kernel(perms, ring, rows, tokens, pos, q_ref, cos_ref, sin_ref, *refs):
    k_refs, v_refs = refs[:ring], refs[ring : 2 * ring]
    out_ref, tk_ref, tv_ref, score_ref = refs[2 * ring :]
    mine = tokens // ring
    base = perms * rows
    scale = HEAD_SIZE ** (-0.5)
    query = jnp.concatenate(
        [
            turned(q_ref[first : first + tokens, :], cos_ref[...], sin_ref[...])
            for first in range(0, q_ref.shape[0], tokens)
        ],
        axis=0,
    ).astype(jnp.bfloat16)
    for kb in range(ring):
        first = pl.multiple_of((pos[1] ^ kb) * mine, mine)
        tk_ref[pl.ds(first, mine), :] = k_refs[kb][base:, :]
        tv_ref[pl.ds(first, mine), :] = v_refs[kb][rows:, :]
    count = q_ref.shape[0]
    tail = (
        lax.dot_general(query, tk_ref[...], ROWS_COLUMNS, preferred_element_type=jnp.float32) * scale
    )
    token = lax.broadcasted_iota(jnp.int32, (count, tokens), 0) & (tokens - 1)
    tail = jnp.where(lax.broadcasted_iota(jnp.int32, (count, tokens), 1) <= token, tail, -1e30)
    tail_top = jnp.max(tail, axis=1, keepdims=True)
    agreed = None
    for r in range(perms):
        top = tail_top
        for kb in range(ring):
            part = (
                lax.dot_general(
                    query,
                    k_refs[kb][r * rows : (r + 1) * rows, :],
                    ROWS_COLUMNS,
                    preferred_element_type=jnp.float32,
                )
                * scale
            )
            score_ref[:, kb * rows : (kb + 1) * rows] = part
            top = jnp.maximum(top, jnp.max(part, axis=1, keepdims=True))
        weights = jnp.exp(tail - top)
        denom = jnp.sum(weights, axis=1, keepdims=True)
        mixed = jnp.dot(
            weights.astype(jnp.bfloat16), tv_ref[...], preferred_element_type=jnp.float32
        )
        for kb in range(ring):
            weights = jnp.exp(score_ref[:, kb * rows : (kb + 1) * rows] - top)
            denom = denom + jnp.sum(weights, axis=1, keepdims=True)
            mixed = mixed + jnp.dot(
                weights.astype(jnp.bfloat16),
                v_refs[kb][:rows, :],
                preferred_element_type=jnp.float32,
            )
        mixed = mixed / denom
        agreed = mixed if agreed is None else agreed + mixed
    out_ref[...] = agreed.astype(out_ref.dtype)


def output_kernel(teams, ring, tokens, pos, *refs):
    y_refs, (w_ref, out_ref, square_ref) = refs[:ring], refs[ring:]
    heads = y_refs[0].shape[1] // tokens
    total = None
    for kb in range(ring):
        for ka in range(teams):
            unit = (pos[0] ^ ka) * ring + (pos[1] ^ kb)
            first = pl.multiple_of(unit * heads * HEAD_SIZE, HEAD_SIZE)
            left = jnp.concatenate(
                [y_refs[kb][ka, j * tokens : (j + 1) * tokens, :] for j in range(heads)], axis=1
            )
            part = jnp.dot(
                left, w_ref[pl.ds(first, heads * HEAD_SIZE), :], preferred_element_type=jnp.float32
            )
            total = part if total is None else total + part
    out_ref[...] = total
    square_ref[...] = lax.dot_general(
        jnp.ones((8, total.shape[1]), jnp.float32),
        total * total,
        ROWS_COLUMNS,
        precision=lax.Precision.HIGHEST,
        preferred_element_type=jnp.float32,
    )


def split_device(
    tail_hidden_states,
    passage_hidden_states,
    lengths,
    storage_order,
    orders,
    w_query,
    key_weight,
    value_weight,
    w_out,
    norm_gain,
):
    shards = lax.axis_size("psg")
    device = lax.axis_index("psg")
    teams = key_weight.shape[1] // HEAD_SIZE
    ring = shards // teams
    tokens, width = tail_hidden_states.shape
    rows = passage_hidden_states.shape[0]
    mine = tokens // ring
    team, seat = device // ring, device % ring
    perms = orders.shape[0]
    heads = w_query.shape[1] // (HEAD_SIZE * shards)
    total_keys = rows * shards
    block = width * ring
    pos = jnp.stack([team, seat]).astype(jnp.int32)

    def swap(x, k):
        return lax.ppermute(x, "psg", [(i, i ^ k) for i in range(shards)])

    def gathered(x):
        pieces, bit = {0: x}, ring // 2
        while bit:
            for kb, piece in list(pieces.items()):
                pieces[kb | bit] = swap(piece, bit)
            bit //= 2
        return [pieces[kb] for kb in range(ring)]

    def exchanged(parts):
        return [swap(part, (ka + 1) * ring) for ka, part in enumerate(parts)]

    def chunk(ka):
        return lax.dynamic_slice_in_dim(passage_hidden_states, (team ^ ka) * block, block, 1)

    others = exchanged([chunk(ka) for ka in range(1, teams)])
    keys_w = gathered(key_weight)
    tails = gathered(tail_hidden_states)
    values_w = gathered(value_weight)

    units = w_query.shape[1] // teams
    part_shape = jax.ShapeDtypeStruct((ring // 2, teams, heads * tokens, HEAD_SIZE), jnp.float32)
    part_spec = pl.BlockSpec((ring // 2, 1, heads * tokens, HEAD_SIZE), lambda i, pos: (0, i, 0, 0))
    keep, send = pl.pallas_call(
        functools.partial(query_kernel, ring, heads),
        name="query_parts",
        compiler_params=granted(10),
        grid_spec=pltpu.PrefetchScalarGridSpec(
            num_scalar_prefetch=1,
            grid=(teams,),
            in_specs=[
                pl.BlockSpec((tokens, width), lambda i, pos: (0, 0)),
                pl.BlockSpec((width, units), lambda i, pos: (0, pos[0] ^ i)),
            ],
            out_specs=[part_spec, part_spec],
            scratch_shapes=[pltpu.VMEM((tokens, units), jnp.float32)],
        ),
        out_shape=[part_shape, part_shape],
        cost_estimate=pl.CostEstimate(
            flops=2 * tokens * width * units * teams,
            bytes_accessed=2 * width * units * teams,
            transcendentals=0,
        ),
    )(pos, tail_hidden_states, w_query)
    bit = 1
    while True:
        query_part = keep + swap(send, bit).astype(jnp.float32)
        bit *= 2
        if bit == ring:
            break
        half = query_part.shape[0] // 2
        keep, send = query_part[:half], query_part[half:].astype(WIRE)
    query_part = query_part[0]

    half = HEAD_SIZE // 2
    freqs = (theta_base ** (-np.arange(half) * 2.0 / HEAD_SIZE)).astype(np.float32)
    key_table = jax.ShapeDtypeStruct((perms * teams * rows + mine, HEAD_SIZE), jnp.float32)
    query_table = jax.ShapeDtypeStruct((tokens, HEAD_SIZE), jnp.float32)
    key_cos, key_sin, query_cos, query_sin = pl.pallas_call(
        functools.partial(table_kernel, teams, ring, rows, perms),
        name="tables",
        compiler_params=granted(6),
        grid_spec=pltpu.PrefetchScalarGridSpec(
            num_scalar_prefetch=4,
            grid=(1,),
            in_specs=in_vmem(1),
            out_specs=in_vmem(4),
        ),
        out_shape=[key_table, key_table, query_table, query_table],
        cost_estimate=pl.CostEstimate(
            flops=key_table.size * 100, bytes_accessed=key_table.size * 8, transcendentals=0
        ),
    )(pos, lengths, storage_order, orders.reshape(-1), jnp.asarray(np.tile(freqs, 2)[None, :]))

    count = teams * rows + mine
    cost = pl.CostEstimate(
        flops=2 * count * block * teams * HEAD_SIZE,
        bytes_accessed=2 * block * (count + teams * HEAD_SIZE),
        transcendentals=0,
    )
    own_shape = jax.ShapeDtypeStruct((count, HEAD_SIZE), jnp.float32)
    acc_shape = pltpu.VMEM((count, teams * HEAD_SIZE), jnp.float32)
    *key_parts, all_rows = pl.pallas_call(
        functools.partial(key_kernel, teams, ring),
        name="key_parts",
        compiler_params=granted(14),
        grid_spec=pltpu.PrefetchScalarGridSpec(
            num_scalar_prefetch=1,
            grid=(1,),
            in_specs=in_vmem(teams + 2 * ring),
            out_specs=in_vmem(teams + 1),
            scratch_shapes=[acc_shape],
        ),
        out_shape=[own_shape] * teams + [jax.ShapeDtypeStruct((count, block), jnp.bfloat16)],
        cost_estimate=cost,
    )(pos, chunk(0), *others, *tails, *keys_w)
    key_others = exchanged([part.astype(WIRE) for part in key_parts[1:]])
    value_parts = pl.pallas_call(
        functools.partial(value_kernel, teams, ring),
        name="value_parts",
        compiler_params=granted(10),
        grid_spec=pltpu.PrefetchScalarGridSpec(
            num_scalar_prefetch=1,
            grid=(1,),
            in_specs=in_vmem(1 + ring),
            out_specs=in_vmem(teams),
            scratch_shapes=[acc_shape],
        ),
        out_shape=[own_shape]
        + [jax.ShapeDtypeStruct(own_shape.shape, jnp.bfloat16)] * (teams - 1),
        cost_estimate=cost,
    )(pos, all_rows, *values_w)
    value_others = exchanged(value_parts[1:])

    def summed(own, others):
        for part in others:
            own = own + part.astype(jnp.float32)
        return own

    key_rows = summed(key_parts[0], key_others)
    turned_keys = pl.pallas_call(
        functools.partial(turn_kernel, perms),
        name="turn_keys",
        compiler_params=granted(6),
        in_specs=in_vmem(3),
        out_specs=pl.BlockSpec(memory_space=pltpu.VMEM),
        out_shape=jax.ShapeDtypeStruct((perms * teams * rows + mine, HEAD_SIZE), jnp.bfloat16),
    )(key_rows, key_cos, key_sin)
    key_pieces = gathered(turned_keys)
    value_rows = summed(value_parts[0], value_others).astype(jnp.bfloat16)
    value_pieces = gathered(value_rows)
    query_others = exchanged([part.astype(WIRE) for part in query_part[1:]])
    query = summed(query_part[0], query_others)

    count = heads * tokens
    attended = pl.pallas_call(
        functools.partial(attend_kernel, perms, ring, teams * rows, tokens),
        name="attend",
        compiler_params=granted(14),
        grid_spec=pltpu.PrefetchScalarGridSpec(
            num_scalar_prefetch=1,
            grid=(1,),
            in_specs=in_vmem(3 + 2 * ring),
            out_specs=pl.BlockSpec(memory_space=pltpu.VMEM),
            scratch_shapes=[
                pltpu.VMEM((tokens, HEAD_SIZE), jnp.bfloat16),
                pltpu.VMEM((tokens, HEAD_SIZE), jnp.bfloat16),
                pltpu.VMEM((count, total_keys), jnp.float32),
            ],
        ),
        out_shape=jax.ShapeDtypeStruct((count, HEAD_SIZE), jnp.bfloat16),
    )(pos, query, query_cos, query_sin, *key_pieces, *value_pieces)

    column = jnp.stack([attended] + exchanged([attended] * (teams - 1)))
    projected, squares = pl.pallas_call(
        functools.partial(output_kernel, teams, ring, tokens),
        name="output_parts",
        compiler_params=granted(12),
        grid_spec=pltpu.PrefetchScalarGridSpec(
            num_scalar_prefetch=1,
            grid=(1,),
            in_specs=in_vmem(ring + 1),
            out_specs=in_vmem(2),
        ),
        out_shape=[
            jax.ShapeDtypeStruct((tokens, w_out.shape[1]), jnp.float32),
            jax.ShapeDtypeStruct((8, tokens), jnp.float32),
        ],
    )(pos, *gathered(column), w_out)
    bit = 1
    while bit < shards:
        squares = squares + swap(squares, bit)
        bit *= 2
    factor = lax.rsqrt(squares[0] / MODEL_WIDTH + epsilon)[:, None]
    return (projected * factor * norm_gain[None, :]).astype(jnp.bfloat16)


def power_of_two(number):
    return number & (number - 1) == 0


def splits(shards, args):
    tail, weight = args[0], args[6]
    teams = weight.shape[1] // HEAD_SIZE
    ring = shards // teams
    return (
        shards % teams == 0
        and power_of_two(shards)
        and power_of_two(teams)
        and ring > 1
        and args[5].shape[1] % (HEAD_SIZE * shards) == 0
        and tail.shape[1] % HEAD_SIZE == 0
        and tail.shape[0] % (16 * ring) == 0
        and power_of_two(tail.shape[0])
        and args[1].shape[0] % 16 == 0
    )


def per_device(*args):
    if splits(lax.axis_size("psg"), args):
        return split_device(*args)
    return general_device(*args)


def solution(mesh):
    placed = (
        P("groups", "psg"),
        P(("groups", "psg"), None),
        P("groups"),
        P("groups"),
        P("groups", None),
        P("psg", None),
        P("psg", None),
        P("psg", None),
        P(None, "psg"),
        P("psg"),
    )
    return jax.shard_map(
        per_device, mesh=mesh, in_specs=placed, out_specs=P("groups", "psg"), check_vma=False
    )
```

profile of v0, /device:TPU:0, one launch (start us, length us, event | category | flops | bytes accessed | tf_op | source)
XLA Modules:
  0.0 119.3 jit_solution(14177901408024304738)
XLA Ops:
  0.0 3.0 %collective-permute-start.9 = (bf16[128,512]{1,0:T(8,128)(2,1)}, bf16[128,512]{1,0:T(8,128)(2,1)}, u32[]{:S(2)}, u32[]{:S(2)}) collective-permute-start(bf16[128,512]{1,0:T(8,128)(2,1)} %refs_4_.2), channel_id=1, source_target_pairs={{0,2},{1,3},{2,0},{3,1},{4,6},{5,7},{6,4},{7,5},{8,10},{9,11},{10,... | collective-permute-start | bytes 393224 | tf_op jit(solution)/shard_map/ppermute | solution.py:392
  3.1 2.1 %constant_dynamic-slice_fusion = (bf16[64,2048]{1,0:T(8,128)(2,1)}, bf16[64,2048]{1,0:T(8,128)(2,1)}, bf16[64,2048]{1,0:T(8,128)(2,1)S(1)}, bf16[64,2048]{1,0:T(8,128)(2,1)}) fusion(bf16[64,8192]{1,0:T(8,128)(2,1)} %param.12, s32[]{:T(128)S(6)} %select_n.28, s32[]{:T(128)S(6)} %select_n.26, s32[]{:T(128)S(6)} %select_n.25, s32[]{:T(128)S(6)} %select_n.27), kind=kLoop, calls=%fused_computation.13 | loop fusion | bytes 2097168 | tf_op jit(solution)/shard_map/dynamic_slice | solution.py:406
  5.2 1.6 %collective-permute-start.5 = (bf16[64,2048]{1,0:T(8,128)(2,1)}, bf16[64,2048]{1,0:T(8,128)(2,1)}, u32[]{:S(2)}, u32[]{:S(2)}) collective-permute-start(bf16[64,2048]{1,0:T(8,128)(2,1)} %get-tuple-element.42), channel_id=1, source_target_pairs={{0,4},{1,5},{2,6},{3,7},{4,0},{5,1},{6,2},{7,3},{8,12},{9,13},{10,... | collective-permute-start | bytes 786440 | tf_op jit(solution)/shard_map/ppermute | solution.py:392
  7.3 1.5 %collective-permute-start.21 = (bf16[512,512]{1,0:T(8,128)(2,1)}, bf16[512,512]{1,0:T(8,128)(2,1)S(1)}, u32[]{:S(2)}, u32[]{:S(2)}) collective-permute-start(bf16[512,512]{1,0:T(8,128)(2,1)} %refs_0_.1), channel_id=1, source_target_pairs={{0,2},{1,3},{2,0},{3,1},{4,6},{5,7},{6,4},{7,5},{8,10},{9,11},{10,... | collective-permute-start | bytes 1572872 | tf_op jit(solution)/shard_map/ppermute | solution.py:392
  8.9 2.2 %copy-done = bf16[512,4096]{1,0:T(8,128)(2,1)S(1)} copy-done((bf16[512,4096]{1,0:T(8,128)(2,1)S(1)}, bf16[512,4096]{1,0:T(8,128)(2,1)}, u32[]{:S(2)}) %copy-start) | copy-done | bytes 4194328
  12.0 3.4 %query_parts.1 = (f32[2,4,256,128]{3,2,1,0:T(8,128)S(1)}, f32[2,4,256,128]{3,2,1,0:T(8,128)}) custom-call(s32[2]{0:T(128)S(1)} %pad_add_fusion.pos, bf16[128,512]{1,0:T(8,128)(2,1)S(1)} %copy-done.2, bf16[512,4096]{1,0:T(8,128)(2,1)S(1)} %copy-done), custom_call_target="tpu_custom_call" | custom-call | flops 536870912 | bytes 4194304 | tf_op jit(solution)/shard_map/query_parts/pallas_call | solution.py:416
  15.4 2.7 %collective-permute-start.6 = (bf16[64,2048]{1,0:T(8,128)(2,1)S(1)}, bf16[64,2048]{1,0:T(8,128)(2,1)S(1)}, u32[]{:S(2)}, u32[]{:S(2)}) collective-permute-start(bf16[64,2048]{1,0:T(8,128)(2,1)S(1)} %copy-done.16), channel_id=1, source_target_pairs={{0,8},{1,9},{2,10},{3,11},{4,12},{5,13},{6,14},{7,15},{8,0},{9,1},... | collective-permute-start | bytes 786440 | tf_op jit(solution)/shard_map/ppermute | solution.py:392
  18.3 17.9 %collective-permute-done.6.refs_2_ = bf16[64,2048]{1,0:T(8,128)(2,1)S(1)} collective-permute-done((bf16[64,2048]{1,0:T(8,128)(2,1)S(1)}, bf16[64,2048]{1,0:T(8,128)(2,1)S(1)}, u32[]{:S(2)}, u32[]{:S(2)}) %collective-permute-start.6) | collective-permute-done | bytes 262176 | tf_op jit(solution)/shard_map/ppermute | solution.py:392
  41.7 2.3 %tables.1 = (f32[800,128]{1,0:T(8,128)S(1)}, f32[800,128]{1,0:T(8,128)S(1)}, f32[128,128]{1,0:T(8,128)S(1)}, f32[128,128]{1,0:T(8,128)S(1)}) custom-call(s32[2]{0:T(128)S(1)} %pad_add_fusion.pos, s32[2]{0:T(128)S(1)} %copy-done.12, s32[2]{0:T(128)S(1)} %copy-done.13, s32[6]{0:T(128)S(1)} %reshape.28.orders, f32[1,128]{1,0:T(1,128)S(1)} %copy-done.14), custom_call_target="tpu_custom_call" | custom-call | flops 10240000 | bytes 819200 | tf_op jit(solution)/shard_map/tables/pallas_call | solution.py:451
  46.9 2.9 %key_parts.1 = (f32[288,128]{1,0:T(8,128)S(1)}, f32[288,128]{1,0:T(8,128)S(1)}, f32[288,128]{1,0:T(8,128)S(1)}, f32[288,128]{1,0:T(8,128)S(1)}, bf16[288,2048]{1,0:T(8,128)(2,1)S(1)}) custom-call(s32[2]{0:T(128)S(1)} %pad_add_fusion.pos, bf16[64,2048]{1,0:T(8,128)(2,1)S(1)} %get-tuple-element.43.refs_0_, bf16[64,2048]{1,0:T(8,128)(2,1)} %collective-permute-done.5.refs_1_, ...), custom_call_target="tpu_custom_call" | custom-call | flops 603979776 | bytes 3276800 | tf_op jit(solution)/shard_map/key_parts/pallas_call | solution.py:475
  49.8 2.6 %value_parts.1 = (f32[288,128]{1,0:T(8,128)S(1)}, bf16[288,128]{1,0:T(8,128)(2,1)S(1)}, bf16[288,128]{1,0:T(8,128)(2,1)S(1)}, bf16[288,128]{1,0:T(8,128)(2,1)S(1)}) custom-call(s32[2]{0:T(128)S(1)} %pad_add_fusion.pos, bf16[288,2048]{1,0:T(8,128)(2,1)S(1)} %get-tuple-element.32.rows_ref, bf16[512,512]{1,0:T(8,128)(2,1)S(1)} %copy-done.5, ...), custom_call_target="tpu_custom_call" | custom-call | flops 603979776 | bytes 3276800 | tf_op jit(solution)/shard_map/value_parts/pallas_call | solution.py:490
  52.4 5.2 %collective-permute-start.23 = (bf16[288,128]{1,0:T(8,128)(2,1)S(1)}, bf16[288,128]{1,0:T(8,128)(2,1)S(1)}, u32[]{:S(2)}, u32[]{:S(2)}) collective-permute-start(bf16[288,128]{1,0:T(8,128)(2,1)S(1)} %get-tuple-element.34), channel_id=1, source_target_pairs={{0,4},{1,5},{2,6},{3,7},{4,0},{5,1},{6,2},{7,3},{8,12},{9,13},{10,... | collective-permute-start | bytes 221192 | tf_op jit(solution)/shard_map/ppermute | solution.py:392
  61.1 2.1 %collective-permute-start.15 = (f16[288,128]{1,0:T(8,128)(2,1)S(1)}, f16[288,128]{1,0:T(8,128)(2,1)S(1)}, u32[]{:S(2)}, u32[]{:S(2)}) collective-permute-start(f16[288,128]{1,0:T(8,128)(2,1)S(1)} %convert_element_type.67), channel_id=1, source_target_pairs={{0,8},{1,9},{2,10},{3,11},{4,12},{5,13},{6,14},{7,15},{8,0},{9,1},... | collective-permute-start | bytes 221192 | tf_op jit(solution)/shard_map/ppermute | solution.py:392
  64.7 1.5 %collective-permute-start.16 = (f16[288,128]{1,0:T(8,128)(2,1)S(1)}, f16[288,128]{1,0:T(8,128)(2,1)S(1)}, u32[]{:S(2)}, u32[]{:S(2)}) collective-permute-start(f16[288,128]{1,0:T(8,128)(2,1)S(1)} %convert_element_type.69), channel_id=1, source_target_pairs={{0,12},{1,13},{2,14},{3,15},{4,8},{5,9},{6,10},{7,11},{8,4},{9,5},... | collective-permute-start | bytes 221192 | tf_op jit(solution)/shard_map/ppermute | solution.py:392
  67.0 1.7 %collective-permute-start.27 = (bf16[288,128]{1,0:T(8,128)(2,1)S(1)}, bf16[288,128]{1,0:T(8,128)(2,1)S(1)}, u32[]{:S(2)}, u32[]{:S(2)}) collective-permute-start(bf16[288,128]{1,0:T(8,128)(2,1)S(1)} %add_convert_fusion.refs_4_), channel_id=1, source_target_pairs={{0,2},{1,3},{2,0},{3,1},{4,6},{5,7},{6,4},{7,5},{8,10},{9,11},{10,... | collective-permute-start | bytes 221192 | tf_op jit(solution)/shard_map/ppermute | solution.py:392
  68.7 4.0 %collective-permute-done.15 = f16[288,128]{1,0:T(8,128)(2,1)S(1)} collective-permute-done((f16[288,128]{1,0:T(8,128)(2,1)S(1)}, f16[288,128]{1,0:T(8,128)(2,1)S(1)}, u32[]{:S(2)}, u32[]{:S(2)}) %collective-permute-start.15) | collective-permute-done | bytes 73760 | tf_op jit(solution)/shard_map/ppermute | solution.py:392
  75.1 2.3 %collective-permute-start.3 = (f16[256,128]{1,0:T(8,128)(2,1)S(1)}, f16[256,128]{1,0:T(8,128)(2,1)S(1)}, u32[]{:S(2)}, u32[]{:S(2)}) collective-permute-start(f16[256,128]{1,0:T(8,128)(2,1)S(1)} %get-tuple-element.47), channel_id=1, source_target_pairs={{0,8},{1,9},{2,10},{3,11},{4,12},{5,13},{6,14},{7,15},{8,0},{9,1},... | collective-permute-start | bytes 196616 | tf_op jit(solution)/shard_map/ppermute | solution.py:392
  79.5 2.3 %collective-permute-done.3 = f16[256,128]{1,0:T(8,128)(2,1)S(1)} collective-permute-done((f16[256,128]{1,0:T(8,128)(2,1)S(1)}, f16[256,128]{1,0:T(8,128)(2,1)S(1)}, u32[]{:S(2)}, u32[]{:S(2)}) %collective-permute-start.3) | collective-permute-done | bytes 65568 | tf_op jit(solution)/shard_map/ppermute | solution.py:392
  81.8 1.7 %collective-permute-done.4 = f16[256,128]{1,0:T(8,128)(2,1)S(1)} collective-permute-done((f16[256,128]{1,0:T(8,128)(2,1)S(1)}, f16[256,128]{1,0:T(8,128)(2,1)S(1)}, u32[]{:S(2)}, u32[]{:S(2)}) %collective-permute-start.4) | collective-permute-done | bytes 65568 | tf_op jit(solution)/shard_map/ppermute | solution.py:392
  83.6 2.5 %attend.1 = bf16[256,128]{1,0:T(8,128)(2,1)S(1)} custom-call(s32[2]{0:T(128)S(1)} %pad_add_fusion.pos, f32[256,128]{1,0:T(8,128)S(1)} %fusion.2.q_ref, f32[128,128]{1,0:T(8,128)S(1)} %get-tuple-element.24.cos_ref, f32[128,128]{1,0:T(8,128)S(1)} %get-tuple-element.25.sin_ref, bf16[800,128]{1,0:T(8,128)(2,1)S(1)} %turn_keys.1.refs_0_, ...), custom_call_target="tpu_custom_call" | custom-call | tf_op jit(solution)/shard_map/attend/pallas_call | solution.py:528
  86.1 3.3 %collective-permute-start.30 = (bf16[256,128]{1,0:T(8,128)(2,1)S(1)}, bf16[256,128]{1,0:T(8,128)(2,1)S(1)}, u32[]{:S(2)}, u32[]{:S(2)}) collective-permute-start(bf16[256,128]{1,0:T(8,128)(2,1)S(1)} %attend.1), channel_id=1, source_target_pairs={{0,8},{1,9},{2,10},{3,11},{4,12},{5,13},{6,14},{7,15},{8,0},{9,1},... | collective-permute-start | bytes 196616 | tf_op jit(solution)/shard_map/ppermute | solution.py:392
  91.2 2.3 %collective-permute-done.30 = bf16[256,128]{1,0:T(8,128)(2,1)S(1)} collective-permute-done((bf16[256,128]{1,0:T(8,128)(2,1)S(1)}, bf16[256,128]{1,0:T(8,128)(2,1)S(1)}, u32[]{:S(2)}, u32[]{:S(2)}) %collective-permute-start.30) | collective-permute-done | bytes 65568 | tf_op jit(solution)/shard_map/ppermute | solution.py:392
  93.5 2.2 %collective-permute-done.31 = bf16[256,128]{1,0:T(8,128)(2,1)S(1)} collective-permute-done((bf16[256,128]{1,0:T(8,128)(2,1)S(1)}, bf16[256,128]{1,0:T(8,128)(2,1)S(1)}, u32[]{:S(2)}, u32[]{:S(2)}) %collective-permute-start.31) | collective-permute-done | bytes 65568 | tf_op jit(solution)/shard_map/ppermute | solution.py:392
  95.6 1.5 %collective-permute-start.33 = (bf16[4,256,128]{2,1,0:T(8,128)(2,1)S(1)}, bf16[4,256,128]{2,1,0:T(8,128)(2,1)S(1)}, u32[]{:S(2)}, u32[]{:S(2)}) collective-permute-start(bf16[4,256,128]{2,1,0:T(8,128)(2,1)S(1)} %pad_maximum_fusion.refs_0_), channel_id=1, source_target_pairs={{0,2},{1,3},{2,0},{3,1},{4,6},{5,7},{6,4},{7,5},{8,10},{9,11},{10,... | collective-permute-start | bytes 786440 | tf_op jit(solution)/shard_map/ppermute | solution.py:392
  97.1 5.2 %collective-permute-done.33.refs_2_ = bf16[4,256,128]{2,1,0:T(8,128)(2,1)S(1)} collective-permute-done((bf16[4,256,128]{2,1,0:T(8,128)(2,1)S(1)}, bf16[4,256,128]{2,1,0:T(8,128)(2,1)S(1)}, u32[]{:S(2)}, u32[]{:S(2)}) %collective-permute-start.33) | collective-permute-done | bytes 262176 | tf_op jit(solution)/shard_map/ppermute | solution.py:392
  102.3 1.5 %collective-permute-done.34.refs_3_ = bf16[4,256,128]{2,1,0:T(8,128)(2,1)S(1)} collective-permute-done((bf16[4,256,128]{2,1,0:T(8,128)(2,1)S(1)}, bf16[4,256,128]{2,1,0:T(8,128)(2,1)S(1)}, u32[]{:S(2)}, u32[]{:S(2)}) %collective-permute-start.34) | collective-permute-done | bytes 262176 | tf_op jit(solution)/shard_map/ppermute | solution.py:392
  103.9 1.7 %output_parts.1 = (f32[128,512]{1,0:T(8,128)S(1)}, f32[8,128]{1,0:T(8,128)S(1)}) custom-call(s32[2]{0:T(128)S(1)} %pad_add_fusion.pos, bf16[4,256,128]{2,1,0:T(8,128)(2,1)S(1)} %pad_maximum_fusion.refs_0_, bf16[4,256,128]{2,1,0:T(8,128)(2,1)S(1)} %collective-permute-done.32.refs_1_, bf16[4,256,128]{2,1,0:T(8,128)(2,1)S(1)} %collective-permute-done.33.refs_2_, ...), custom_call_target="tpu_custom_call" | custom-call | tf_op jit(solution)/shard_map/output_parts/pallas_call | solution.py:547
  106.8 1.4 %collective-permute-start.36 = (f32[8,128]{1,0:T(8,128)S(1)}, f32[8,128]{1,0:T(8,128)S(1)}, u32[]{:S(2)}, u32[]{:S(2)}) collective-permute-start(f32[8,128]{1,0:T(8,128)S(1)} %add.89), channel_id=1, source_target_pairs={{0,2},{1,3},{2,0},{3,1},{4,6},{5,7},{6,4},{7,5},{8,10},{9,11},{10,... | collective-permute-start | bytes 12296 | tf_op jit(solution)/shard_map/ppermute | solution.py:392
  108.2 2.2 %collective-permute-done.36 = f32[8,128]{1,0:T(8,128)S(1)} collective-permute-done((f32[8,128]{1,0:T(8,128)S(1)}, f32[8,128]{1,0:T(8,128)S(1)}, u32[]{:S(2)}, u32[]{:S(2)}) %collective-permute-start.36) | collective-permute-done | bytes 4128 | tf_op jit(solution)/shard_map/ppermute | solution.py:392
  111.6 2.4 %collective-permute-done.37 = f32[8,128]{1,0:T(8,128)S(1)} collective-permute-done((f32[8,128]{1,0:T(8,128)S(1)}, f32[8,128]{1,0:T(8,128)S(1)}, u32[]{:S(2)}, u32[]{:S(2)}) %collective-permute-start.37) | collective-permute-done | bytes 4128 | tf_op jit(solution)/shard_map/ppermute | solution.py:392
  114.0 2.2 %collective-permute-start.38 = (f32[8,128]{1,0:T(8,128)S(1)}, f32[8,128]{1,0:T(8,128)S(1)}, u32[]{:S(2)}, u32[]{:S(2)}) collective-permute-start(f32[8,128]{1,0:T(8,128)S(1)} %add.91), channel_id=1, source_target_pairs={{0,8},{1,9},{2,10},{3,11},{4,12},{5,13},{6,14},{7,15},{8,0},{9,1},... | collective-permute-start | bytes 12296 | tf_op jit(solution)/shard_map/ppermute | solution.py:392
  116.2 2.3 %collective-permute-done.38 = f32[8,128]{1,0:T(8,128)S(1)} collective-permute-done((f32[8,128]{1,0:T(8,128)S(1)}, f32[8,128]{1,0:T(8,128)S(1)}, u32[]{:S(2)}, u32[]{:S(2)}) %collective-permute-start.38) | collective-permute-done | bytes 4128 | tf_op jit(solution)/shard_map/ppermute | solution.py:392
  (112 shorter events, 25.6 us)
Async XLA Ops:
  0.0 15.3 %collective-permute-start.9 = (bf16[128,512]{1,0:T(8,128)(2,1)}, bf16[128,512]{1,0:T(8,128)(2,1)}, u32[]{:S(2)}, u32[]{:S(2)}) collective-permute-start(bf16[128,512]{1,0:T(8,128)(2,1)} %refs_4_.2), channel_id=1, source_target_pairs={{0,2},{1,3},{2,0},{3,1},{4,6},{5,7},{6,4},{7,5},{8,10},{9,11},{10,... | collective-permute-start | bytes 393224 | tf_op jit(solution)/shard_map/ppermute | solution.py:392
  3.1 12.3 %collective-permute-start.8 = (bf16[128,512]{1,0:T(8,128)(2,1)}, bf16[128,512]{1,0:T(8,128)(2,1)}, u32[]{:S(2)}, u32[]{:S(2)}) collective-permute-start(bf16[128,512]{1,0:T(8,128)(2,1)} %refs_4_.2), channel_id=1, source_target_pairs={{0,1},{1,0},{2,3},{3,2},{4,5},{5,4},{6,7},{7,6},{8,9},{9,8},{10,11... | collective-permute-start | bytes 393224 | tf_op jit(solution)/shard_map/ppermute | solution.py:392
  5.2 12.9 %collective-permute-start.5 = (bf16[64,2048]{1,0:T(8,128)(2,1)}, bf16[64,2048]{1,0:T(8,128)(2,1)}, u32[]{:S(2)}, u32[]{:S(2)}) collective-permute-start(bf16[64,2048]{1,0:T(8,128)(2,1)} %get-tuple-element.42), channel_id=1, source_target_pairs={{0,4},{1,5},{2,6},{3,7},{4,0},{5,1},{6,2},{7,3},{8,12},{9,13},{10,... | collective-permute-start | bytes 786440 | tf_op jit(solution)/shard_map/ppermute | solution.py:392
  6.8 31.4 %collective-permute-start.12 = (bf16[512,512]{1,0:T(8,128)(2,1)}, bf16[512,512]{1,0:T(8,128)(2,1)S(1)}, u32[]{:S(2)}, u32[]{:S(2)}) collective-permute-start(bf16[512,512]{1,0:T(8,128)(2,1)} %refs_8_.1), channel_id=1, source_target_pairs={{0,2},{1,3},{2,0},{3,1},{4,6},{5,7},{6,4},{7,5},{8,10},{9,11},{10,... | collective-permute-start | bytes 1572872 | tf_op jit(solution)/shard_map/ppermute | solution.py:392
  7.3 32.0 %collective-permute-start.21 = (bf16[512,512]{1,0:T(8,128)(2,1)}, bf16[512,512]{1,0:T(8,128)(2,1)S(1)}, u32[]{:S(2)}, u32[]{:S(2)}) collective-permute-start(bf16[512,512]{1,0:T(8,128)(2,1)} %refs_0_.1), channel_id=1, source_target_pairs={{0,2},{1,3},{2,0},{3,1},{4,6},{5,7},{6,4},{7,5},{8,10},{9,11},{10,... | collective-permute-start | bytes 1572872 | tf_op jit(solution)/shard_map/ppermute | solution.py:392
  15.4 45.8 %collective-permute-start = (f32[2,4,256,128]{3,2,1,0:T(8,128)}, f32[2,4,256,128]{3,2,1,0:T(8,128)}, u32[]{:S(2)}, u32[]{:S(2)}) collective-permute-start(f32[2,4,256,128]{3,2,1,0:T(8,128)} %get-tuple-element.23), channel_id=1, source_target_pairs={{0,1},{1,0},{2,3},{3,2},{4,5},{5,4},{6,7},{7,6},{8,9},{9,8},{10,11... | collective-permute-start | bytes 3145736 | tf_op jit(solution)/shard_map/ppermute | solution.py:392
  15.4 20.8 %collective-permute-start.6 = (bf16[64,2048]{1,0:T(8,128)(2,1)S(1)}, bf16[64,2048]{1,0:T(8,128)(2,1)S(1)}, u32[]{:S(2)}, u32[]{:S(2)}) collective-permute-start(bf16[64,2048]{1,0:T(8,128)(2,1)S(1)} %copy-done.16), channel_id=1, source_target_pairs={{0,8},{1,9},{2,10},{3,11},{4,12},{5,13},{6,14},{7,15},{8,0},{9,1},... | collective-permute-start | bytes 786440 | tf_op jit(solution)/shard_map/ppermute | solution.py:392
  18.1 18.9 %collective-permute-start.7 = (bf16[64,2048]{1,0:T(8,128)(2,1)S(1)}, bf16[64,2048]{1,0:T(8,128)(2,1)S(1)}, u32[]{:S(2)}, u32[]{:S(2)}) collective-permute-start(bf16[64,2048]{1,0:T(8,128)(2,1)S(1)} %copy-done.15), channel_id=1, source_target_pairs={{0,12},{1,13},{2,14},{3,15},{4,8},{5,9},{6,10},{7,11},{8,4},{9,5},... | collective-permute-start | bytes 786440 | tf_op jit(solution)/shard_map/ppermute | solution.py:392
  37.6 6.4 %collective-permute-start.11 = (bf16[512,512]{1,0:T(8,128)(2,1)S(1)}, bf16[512,512]{1,0:T(8,128)(2,1)}, u32[]{:S(2)}, u32[]{:S(2)}) collective-permute-start(bf16[512,512]{1,0:T(8,128)(2,1)S(1)} %copy-done.4), channel_id=1, source_target_pairs={{0,1},{1,0},{2,3},{3,2},{4,5},{5,4},{6,7},{7,6},{8,9},{9,8},{10,11... | collective-permute-start | bytes 1572872 | tf_op jit(solution)/shard_map/ppermute | solution.py:392
  38.1 5.9 %collective-permute-start.13 = (bf16[512,512]{1,0:T(8,128)(2,1)S(1)}, bf16[512,512]{1,0:T(8,128)(2,1)}, u32[]{:S(2)}, u32[]{:S(2)}) collective-permute-start(bf16[512,512]{1,0:T(8,128)(2,1)S(1)} %collective-permute-done.12.refs_10_), channel_id=1, source_target_pairs={{0,1},{1,0},{2,3},{3,2},{4,5},{5,4},{6,7},{7,6},{8,9},{9,8},{10,11... | collective-permute-start | bytes 1572872 | tf_op jit(solution)/shard_map/ppermute | solution.py:392
  39.1 10.6 %collective-permute-start.20 = (bf16[512,512]{1,0:T(8,128)(2,1)S(1)}, bf16[512,512]{1,0:T(8,128)(2,1)}, u32[]{:S(2)}, u32[]{:S(2)}) collective-permute-start(bf16[512,512]{1,0:T(8,128)(2,1)S(1)} %copy-done.5), channel_id=1, source_target_pairs={{0,1},{1,0},{2,3},{3,2},{4,5},{5,4},{6,7},{7,6},{8,9},{9,8},{10,11... | collective-permute-start | bytes 1572872 | tf_op jit(solution)/shard_map/ppermute | solution.py:392
  39.3 10.4 %collective-permute-start.22 = (bf16[512,512]{1,0:T(8,128)(2,1)S(1)}, bf16[512,512]{1,0:T(8,128)(2,1)}, u32[]{:S(2)}, u32[]{:S(2)}) collective-permute-start(bf16[512,512]{1,0:T(8,128)(2,1)S(1)} %collective-permute-done.21.refs_2_), channel_id=1, source_target_pairs={{0,1},{1,0},{2,3},{3,2},{4,5},{5,4},{6,7},{7,6},{8,9},{9,8},{10,11... | collective-permute-start | bytes 1572872 | tf_op jit(solution)/shard_map/ppermute | solution.py:392
  52.4 12.3 %collective-permute-start.23 = (bf16[288,128]{1,0:T(8,128)(2,1)S(1)}, bf16[288,128]{1,0:T(8,128)(2,1)S(1)}, u32[]{:S(2)}, u32[]{:S(2)}) collective-permute-start(bf16[288,128]{1,0:T(8,128)(2,1)S(1)} %get-tuple-element.34), channel_id=1, source_target_pairs={{0,4},{1,5},{2,6},{3,7},{4,0},{5,1},{6,2},{7,3},{8,12},{9,13},{10,... | collective-permute-start | bytes 221192 | tf_op jit(solution)/shard_map/ppermute | solution.py:392
  57.5 9.0 %collective-permute-start.24 = (bf16[288,128]{1,0:T(8,128)(2,1)S(1)}, bf16[288,128]{1,0:T(8,128)(2,1)S(1)}, u32[]{:S(2)}, u32[]{:S(2)}) collective-permute-start(bf16[288,128]{1,0:T(8,128)(2,1)S(1)} %get-tuple-element.35), channel_id=1, source_target_pairs={{0,8},{1,9},{2,10},{3,11},{4,12},{5,13},{6,14},{7,15},{8,0},{9,1},... | collective-permute-start | bytes 221192 | tf_op jit(solution)/shard_map/ppermute | solution.py:392
  58.7 8.3 %collective-permute-start.25 = (bf16[288,128]{1,0:T(8,128)(2,1)S(1)}, bf16[288,128]{1,0:T(8,128)(2,1)S(1)}, u32[]{:S(2)}, u32[]{:S(2)}) collective-permute-start(bf16[288,128]{1,0:T(8,128)(2,1)S(1)} %get-tuple-element.36), channel_id=1, source_target_pairs={{0,12},{1,13},{2,14},{3,15},{4,8},{5,9},{6,10},{7,11},{8,4},{9,5},... | collective-permute-start | bytes 221192 | tf_op jit(solution)/shard_map/ppermute | solution.py:392
  60.1 8.6 %collective-permute-start.14 = (f16[288,128]{1,0:T(8,128)(2,1)S(1)}, f16[288,128]{1,0:T(8,128)(2,1)S(1)}, u32[]{:S(2)}, u32[]{:S(2)}) collective-permute-start(f16[288,128]{1,0:T(8,128)(2,1)S(1)} %convert_element_type.65), channel_id=1, source_target_pairs={{0,4},{1,5},{2,6},{3,7},{4,0},{5,1},{6,2},{7,3},{8,12},{9,13},{10,... | collective-permute-start | bytes 221192 | tf_op jit(solution)/shard_map/ppermute | solution.py:392
  61.1 11.5 %collective-permute-start.15 = (f16[288,128]{1,0:T(8,128)(2,1)S(1)}, f16[288,128]{1,0:T(8,128)(2,1)S(1)}, u32[]{:S(2)}, u32[]{:S(2)}) collective-permute-start(f16[288,128]{1,0:T(8,128)(2,1)S(1)} %convert_element_type.67), channel_id=1, source_target_pairs={{0,8},{1,9},{2,10},{3,11},{4,12},{5,13},{6,14},{7,15},{8,0},{9,1},... | collective-permute-start | bytes 221192 | tf_op jit(solution)/shard_map/ppermute | solution.py:392
  64.7 7.9 %collective-permute-start.16 = (f16[288,128]{1,0:T(8,128)(2,1)S(1)}, f16[288,128]{1,0:T(8,128)(2,1)S(1)}, u32[]{:S(2)}, u32[]{:S(2)}) collective-permute-start(f16[288,128]{1,0:T(8,128)(2,1)S(1)} %convert_element_type.69), channel_id=1, source_target_pairs={{0,12},{1,13},{2,14},{3,15},{4,8},{5,9},{6,10},{7,11},{8,4},{9,5},... | collective-permute-start | bytes 221192 | tf_op jit(solution)/shard_map/ppermute | solution.py:392
  66.5 7.3 %collective-permute-start.1 = (f16[1,4,256,128]{3,2,1,0:T(8,128)(2,1)S(1)}, f16[1,4,256,128]{3,2,1,0:T(8,128)(2,1)S(1)}, u32[]{:S(2)}, u32[]{:S(2)}) collective-permute-start(f16[1,4,256,128]{3,2,1,0:T(8,128)(2,1)S(1)} %slice_convert_fusion), channel_id=1, source_target_pairs={{0,2},{1,3},{2,0},{3,1},{4,6},{5,7},{6,4},{7,5},{8,10},{9,11},{10,... | collective-permute-start | bytes 786440 | tf_op jit(solution)/shard_map/ppermute | solution.py:392
  67.0 11.4 %collective-permute-start.27 = (bf16[288,128]{1,0:T(8,128)(2,1)S(1)}, bf16[288,128]{1,0:T(8,128)(2,1)S(1)}, u32[]{:S(2)}, u32[]{:S(2)}) collective-permute-start(bf16[288,128]{1,0:T(8,128)(2,1)S(1)} %add_convert_fusion.refs_4_), channel_id=1, source_target_pairs={{0,2},{1,3},{2,0},{3,1},{4,6},{5,7},{6,4},{7,5},{8,10},{9,11},{10,... | collective-permute-start | bytes 221192 | tf_op jit(solution)/shard_map/ppermute | solution.py:392
  72.9 6.1 %collective-permute-start.18 = (bf16[800,128]{1,0:T(8,128)(2,1)S(1)}, bf16[800,128]{1,0:T(8,128)(2,1)S(1)}, u32[]{:S(2)}, u32[]{:S(2)}) collective-permute-start(bf16[800,128]{1,0:T(8,128)(2,1)S(1)} %turn_keys.1.refs_0_), channel_id=1, source_target_pairs={{0,2},{1,3},{2,0},{3,1},{4,6},{5,7},{6,4},{7,5},{8,10},{9,11},{10,... | collective-permute-start | bytes 614408 | tf_op jit(solution)/shard_map/ppermute | solution.py:392
  74.0 5.0 %collective-permute-start.2 = (f16[256,128]{1,0:T(8,128)(2,1)S(1)}, f16[256,128]{1,0:T(8,128)(2,1)S(1)}, u32[]{:S(2)}, u32[]{:S(2)}) collective-permute-start(f16[256,128]{1,0:T(8,128)(2,1)S(1)} %get-tuple-element.45), channel_id=1, source_target_pairs={{0,4},{1,5},{2,6},{3,7},{4,0},{5,1},{6,2},{7,3},{8,12},{9,13},{10,... | collective-permute-start | bytes 196616 | tf_op jit(solution)/shard_map/ppermute | solution.py:392
  75.1 6.7 %collective-permute-start.3 = (f16[256,128]{1,0:T(8,128)(2,1)S(1)}, f16[256,128]{1,0:T(8,128)(2,1)S(1)}, u32[]{:S(2)}, u32[]{:S(2)}) collective-permute-start(f16[256,128]{1,0:T(8,128)(2,1)S(1)} %get-tuple-element.47), channel_id=1, source_target_pairs={{0,8},{1,9},{2,10},{3,11},{4,12},{5,13},{6,14},{7,15},{8,0},{9,1},... | collective-permute-start | bytes 196616 | tf_op jit(solution)/shard_map/ppermute | solution.py:392
  77.4 6.1 %collective-permute-start.4 = (f16[256,128]{1,0:T(8,128)(2,1)S(1)}, f16[256,128]{1,0:T(8,128)(2,1)S(1)}, u32[]{:S(2)}, u32[]{:S(2)}) collective-permute-start(f16[256,128]{1,0:T(8,128)(2,1)S(1)} %get-tuple-element.46), channel_id=1, source_target_pairs={{0,12},{1,13},{2,14},{3,15},{4,8},{5,9},{6,10},{7,11},{8,4},{9,5},... | collective-permute-start | bytes 196616 | tf_op jit(solution)/shard_map/ppermute | solution.py:392
  78.4 5.1 %collective-permute-start.26 = (bf16[288,128]{1,0:T(8,128)(2,1)S(1)}, bf16[288,128]{1,0:T(8,128)(2,1)S(1)}, u32[]{:S(2)}, u32[]{:S(2)}) collective-permute-start(bf16[288,128]{1,0:T(8,128)(2,1)S(1)} %add_convert_fusion.refs_4_), channel_id=1, source_target_pairs={{0,1},{1,0},{2,3},{3,2},{4,5},{5,4},{6,7},{7,6},{8,9},{9,8},{10,11... | collective-permute-start | bytes 221192 | tf_op jit(solution)/shard_map/ppermute | solution.py:392
  79.0 4.6 %collective-permute-start.17 = (bf16[800,128]{1,0:T(8,128)(2,1)S(1)}, bf16[800,128]{1,0:T(8,128)(2,1)S(1)}, u32[]{:S(2)}, u32[]{:S(2)}) collective-permute-start(bf16[800,128]{1,0:T(8,128)(2,1)S(1)} %turn_keys.1.refs_0_), channel_id=1, source_target_pairs={{0,1},{1,0},{2,3},{3,2},{4,5},{5,4},{6,7},{7,6},{8,9},{9,8},{10,11... | collective-permute-start | bytes 614408 | tf_op jit(solution)/shard_map/ppermute | solution.py:392
  79.0 4.6 %collective-permute-start.28 = (bf16[288,128]{1,0:T(8,128)(2,1)S(1)}, bf16[288,128]{1,0:T(8,128)(2,1)S(1)}, u32[]{:S(2)}, u32[]{:S(2)}) collective-permute-start(bf16[288,128]{1,0:T(8,128)(2,1)S(1)} %collective-permute-done.27.refs_6_), channel_id=1, source_target_pairs={{0,1},{1,0},{2,3},{3,2},{4,5},{5,4},{6,7},{7,6},{8,9},{9,8},{10,11... | collective-permute-start | bytes 221192 | tf_op jit(solution)/shard_map/ppermute | solution.py:392
  86.1 5.1 %collective-permute-start.29 = (bf16[256,128]{1,0:T(8,128)(2,1)S(1)}, bf16[256,128]{1,0:T(8,128)(2,1)S(1)}, u32[]{:S(2)}, u32[]{:S(2)}) collective-permute-start(bf16[256,128]{1,0:T(8,128)(2,1)S(1)} %attend.1), channel_id=1, source_target_pairs={{0,4},{1,5},{2,6},{3,7},{4,0},{5,1},{6,2},{7,3},{8,12},{9,13},{10,... | collective-permute-start | bytes 196616 | tf_op jit(solution)/shard_map/ppermute | solution.py:392
  86.1 7.3 %collective-permute-start.30 = (bf16[256,128]{1,0:T(8,128)(2,1)S(1)}, bf16[256,128]{1,0:T(8,128)(2,1)S(1)}, u32[]{:S(2)}, u32[]{:S(2)}) collective-permute-start(bf16[256,128]{1,0:T(8,128)(2,1)S(1)} %attend.1), channel_id=1, source_target_pairs={{0,8},{1,9},{2,10},{3,11},{4,12},{5,13},{6,14},{7,15},{8,0},{9,1},... | collective-permute-start | bytes 196616 | tf_op jit(solution)/shard_map/ppermute | solution.py:392
  89.4 6.2 %collective-permute-start.31 = (bf16[256,128]{1,0:T(8,128)(2,1)S(1)}, bf16[256,128]{1,0:T(8,128)(2,1)S(1)}, u32[]{:S(2)}, u32[]{:S(2)}) collective-permute-start(bf16[256,128]{1,0:T(8,128)(2,1)S(1)} %attend.1), channel_id=1, source_target_pairs={{0,12},{1,13},{2,14},{3,15},{4,8},{5,9},{6,10},{7,11},{8,4},{9,5},... | collective-permute-start | bytes 196616 | tf_op jit(solution)/shard_map/ppermute | solution.py:392
  95.6 6.7 %collective-permute-start.33 = (bf16[4,256,128]{2,1,0:T(8,128)(2,1)S(1)}, bf16[4,256,128]{2,1,0:T(8,128)(2,1)S(1)}, u32[]{:S(2)}, u32[]{:S(2)}) collective-permute-start(bf16[4,256,128]{2,1,0:T(8,128)(2,1)S(1)} %pad_maximum_fusion.refs_0_), channel_id=1, source_target_pairs={{0,2},{1,3},{2,0},{3,1},{4,6},{5,7},{6,4},{7,5},{8,10},{9,11},{10,... | collective-permute-start | bytes 786440 | tf_op jit(solution)/shard_map/ppermute | solution.py:392
  97.1 5.2 %collective-permute-start.32 = (bf16[4,256,128]{2,1,0:T(8,128)(2,1)S(1)}, bf16[4,256,128]{2,1,0:T(8,128)(2,1)S(1)}, u32[]{:S(2)}, u32[]{:S(2)}) collective-permute-start(bf16[4,256,128]{2,1,0:T(8,128)(2,1)S(1)} %pad_maximum_fusion.refs_0_), channel_id=1, source_target_pairs={{0,1},{1,0},{2,3},{3,2},{4,5},{5,4},{6,7},{7,6},{8,9},{9,8},{10,11... | collective-permute-start | bytes 786440 | tf_op jit(solution)/shard_map/ppermute | solution.py:392
  (26 other events, 362.3 us)
where the time goes:
time: 120 us; the launch traced here: 119 us
  waiting for transfers between devices  47.2 us (39%)
  starting transfers between devices  41.5 us (35%)
  Pallas kernels  15.5 us (13%)
  local copies, waits for them, and re-layouts  12.2 us (10%)
  other arithmetic  2.5 us (2%)
    ppermute x39, waiting for transfers between devices, swap(): return lax.ppermute(x, 'psg', [(i, i ^ k) for i in range(shards)])  47.2 us
    ppermute x39, starting transfers between devices, swap(): return lax.ppermute(x, 'psg', [(i, i ^ k) for i in range(shards)])  41.5 us
    unnamed x39, local copies, waits for them, and re-layouts  9.34 us
    pallas_call x1, Pallas kernels, split_device(): pl.pallas_call(functools.partial(query_kernel, ring, heads), name='query_...  3.4 us
    pallas_call x1, Pallas kernels, split_device(): pl.pallas_call(functools.partial(key_kernel, teams, ring), name='key_part...  2.87 us
    pallas_call x1, Pallas kernels, split_device(): pl.pallas_call(functools.partial(value_kernel, teams, ring), name='value_...  2.6 us
    pallas_call x1, Pallas kernels, split_device(): pl.pallas_call(functools.partial(attend_kernel, perms, ring, teams * rows...  2.47 us
  transfers between devices with their start and end apart: 39, of which 17 were waited for; matrix products, arithmetic and copies ran while one was open for 4% of the time, Pallas kernels for 10%

commit v1 on v0

--- a/solution.py
+++ b/solution.py
@@ -167,6 +167,10 @@
     return pltpu.CompilerParams(vmem_limit_bytes=mebibytes << 20)
 
 
+def team_at(team, steps, teams):
+    return (team + steps) & (teams - 1)
+
+
 def in_vmem(count):
     return [pl.BlockSpec(memory_space=pltpu.VMEM)] * count
 
@@ -245,7 +249,7 @@
         total = part if total is None else total + part
     acc_ref[...] = total
     for ka in range(teams):
-        column = pl.multiple_of((pos[0] ^ ka) * HEAD_SIZE, HEAD_SIZE)
+        column = pl.multiple_of(team_at(pos[0], ka, teams) * HEAD_SIZE, HEAD_SIZE)
         out_refs[ka][...] = acc_ref[:, pl.ds(column, HEAD_SIZE)].astype(out_refs[ka].dtype)
 
 
@@ -257,7 +261,7 @@
         column = pl.multiple_of((pos[1] ^ kb) * width, width)
         place = slice(kb * width, (kb + 1) * width)
         for ka in range(teams):
-            first = pl.multiple_of((pos[0] ^ ka) * rows, rows)
+            first = pl.multiple_of(team_at(pos[0], -ka, teams) * rows, rows)
             all_ref[pl.ds(first, rows), place] = x_refs[ka][:, pl.ds(column, width)]
         first = pl.multiple_of(pos[1] * mine, mine)
         all_ref[teams * rows :, place] = t_refs[kb][pl.ds(first, mine), :]
@@ -337,23 +341,25 @@
     out_ref[...] = agreed.astype(out_ref.dtype)
 
 
-def output_kernel(teams, ring, tokens, pos, *refs):
-    y_refs, (w_ref, out_ref, square_ref) = refs[:ring], refs[ring:]
-    heads = y_refs[0].shape[1] // tokens
-    total = None
-    for kb in range(ring):
-        for ka in range(teams):
-            unit = (pos[0] ^ ka) * ring + (pos[1] ^ kb)
-            first = pl.multiple_of(unit * heads * HEAD_SIZE, HEAD_SIZE)
-            left = jnp.concatenate(
-                [y_refs[kb][ka, j * tokens : (j + 1) * tokens, :] for j in range(heads)], axis=1
-            )
-            part = jnp.dot(
-                left, w_ref[pl.ds(first, heads * HEAD_SIZE), :], preferred_element_type=jnp.float32
-            )
-            total = part if total is None else total + part
-    out_ref[...] = total
-    square_ref[...] = lax.dot_general(
+def output_kernel(units, teams, ring, tokens, first_part, pos, *refs):
+    y_refs, w_ref, refs = refs[: len(units)], refs[len(units)], refs[len(units) + 1 :]
+    heads = y_refs[0].shape[0] // tokens
+    total = None if first_part else refs[0][...]
+    for (kb, ka), y_ref in zip(units, y_refs, strict=True):
+        unit = team_at(pos[0], -ka, teams) * ring + (pos[1] ^ kb)
+        first = pl.multiple_of(unit * heads * HEAD_SIZE, HEAD_SIZE)
+        left = jnp.concatenate(
+            [y_ref[j * tokens : (j + 1) * tokens, :] for j in range(heads)], axis=1
+        )
+        part = jnp.dot(
+            left, w_ref[pl.ds(first, heads * HEAD_SIZE), :], preferred_element_type=jnp.float32
+        )
+        total = part if total is None else total + part
+    if first_part:
+        refs[0][...] = total
+        return
+    refs[1][...] = total
+    refs[2][...] = lax.dot_general(
         jnp.ones((8, total.shape[1]), jnp.float32),
         total * total,
         ROWS_COLUMNS,
@@ -400,12 +406,19 @@
         return [pieces[kb] for kb in range(ring)]
 
     def exchanged(parts):
-        return [swap(part, (ka + 1) * ring) for ka, part in enumerate(parts)]
-
-    def chunk(ka):
-        return lax.dynamic_slice_in_dim(passage_hidden_states, (team ^ ka) * block, block, 1)
-
-    others = exchanged([chunk(ka) for ka in range(1, teams)])
+        moved = []
+        for ka, part in enumerate(parts, 1):
+            pairs = [(i, (i + ka * ring) % shards) for i in range(shards)]
+            moved.append(lax.ppermute(part, "psg", pairs))
+        return moved
+
+    chunks = [
+        lax.dynamic_slice_in_dim(
+            passage_hidden_states, team_at(team, ka, teams) * block, block, 1
+        )
+        for ka in range(teams)
+    ]
+    others = exchanged(chunks[1:])
     keys_w = gathered(key_weight)
     tails = gathered(tail_hidden_states)
     values_w = gathered(value_weight)
@@ -415,14 +428,14 @@
     part_spec = pl.BlockSpec((ring // 2, 1, heads * tokens, HEAD_SIZE), lambda i, pos: (0, i, 0, 0))
     keep, send = pl.pallas_call(
         functools.partial(query_kernel, ring, heads),
-        name="query_parts",
+        name="qp",
         compiler_params=granted(10),
         grid_spec=pltpu.PrefetchScalarGridSpec(
             num_scalar_prefetch=1,
             grid=(teams,),
             in_specs=[
                 pl.BlockSpec((tokens, width), lambda i, pos: (0, 0)),
-                pl.BlockSpec((width, units), lambda i, pos: (0, pos[0] ^ i)),
+                pl.BlockSpec((width, units), lambda i, pos: (0, team_at(pos[0], i, teams))),
             ],
             out_specs=[part_spec, part_spec],
             scratch_shapes=[pltpu.VMEM((tokens, units), jnp.float32)],
@@ -433,10 +446,11 @@
             bytes_accessed=2 * width * units * teams,
             transcendentals=0,
         ),
-    )(pos, tail_hidden_states, w_query)
+    )(pos, tail_hidden_states, pltpu.with_memory_space_constraint(w_query, pltpu.HBM))
     bit = 1
     while True:
-        query_part = keep + swap(send, bit).astype(jnp.float32)
+        arrived = swap(send, bit)
+        query_part = keep + arrived.astype(jnp.float32)
         bit *= 2
         if bit == ring:
             break
@@ -450,7 +464,7 @@
     query_table = jax.ShapeDtypeStruct((tokens, HEAD_SIZE), jnp.float32)
     key_cos, key_sin, query_cos, query_sin = pl.pallas_call(
         functools.partial(table_kernel, teams, ring, rows, perms),
-        name="tables",
+        name="tab",
         compiler_params=granted(6),
         grid_spec=pltpu.PrefetchScalarGridSpec(
             num_scalar_prefetch=4,
@@ -474,7 +488,7 @@
     acc_shape = pltpu.VMEM((count, teams * HEAD_SIZE), jnp.float32)
     *key_parts, all_rows = pl.pallas_call(
         functools.partial(key_kernel, teams, ring),
-        name="key_parts",
+        name="kp",
         compiler_params=granted(14),
         grid_spec=pltpu.PrefetchScalarGridSpec(
             num_scalar_prefetch=1,
@@ -485,11 +499,11 @@
         ),
         out_shape=[own_shape] * teams + [jax.ShapeDtypeStruct((count, block), jnp.bfloat16)],
         cost_estimate=cost,
-    )(pos, chunk(0), *others, *tails, *keys_w)
+    )(pos, chunks[0], *others, *tails, *keys_w)
     key_others = exchanged([part.astype(WIRE) for part in key_parts[1:]])
     value_parts = pl.pallas_call(
         functools.partial(value_kernel, teams, ring),
-        name="value_parts",
+        name="vp",
         compiler_params=granted(10),
         grid_spec=pltpu.PrefetchScalarGridSpec(
             num_scalar_prefetch=1,
@@ -512,7 +526,7 @@
     key_rows = summed(key_parts[0], key_others)
     turned_keys = pl.pallas_call(
         functools.partial(turn_kernel, perms),
-        name="turn_keys",
+        name="turn",
         compiler_params=granted(6),
         in_specs=in_vmem(3),
         out_specs=pl.BlockSpec(memory_space=pltpu.VMEM),
@@ -543,22 +557,36 @@
         out_shape=jax.ShapeDtypeStruct((count, HEAD_SIZE), jnp.bfloat16),
     )(pos, query, query_cos, query_sin, *key_pieces, *value_pieces)
 
-    column = jnp.stack([attended] + exchanged([attended] * (teams - 1)))
-    projected, squares = pl.pallas_call(
-        functools.partial(output_kernel, teams, ring, tokens),
-        name="output_parts",
-        compiler_params=granted(12),
-        grid_spec=pltpu.PrefetchScalarGridSpec(
-            num_scalar_prefetch=1,
-            grid=(1,),
-            in_specs=in_vmem(ring + 1),
-            out_specs=in_vmem(2),
-        ),
-        out_shape=[
-            jax.ShapeDtypeStruct((tokens, w_out.shape[1]), jnp.float32),
-            jax.ShapeDtypeStruct((8, tokens), jnp.float32),
-        ],
-    )(pos, *gathered(column), w_out)
+    pieces, bit = {(0, 0): attended}, ring // 2
+    ahead = swap(attended, bit)
+    for ka, piece in enumerate(exchanged([attended] * (teams - 1))):
+        pieces[0, ka + 1] = piece
+    for (kb, ka), piece in list(pieces.items()):
+        pieces[kb | bit, ka] = ahead if ka == 0 else swap(piece, bit)
+    while bit > 1:
+        bit //= 2
+        for (kb, ka), piece in list(pieces.items()):
+            pieces[kb | bit, ka] = swap(piece, bit)
+
+    late = [(kb, ka) for kb, ka in pieces if ka == teams // 2 and kb & (ring // 2)]
+    early = [unit for unit in pieces if unit not in late]
+
+    def output(units, before):
+        projected_shape = jax.ShapeDtypeStruct((tokens, w_out.shape[1]), jnp.float32)
+        shapes = [projected_shape] + [jax.ShapeDtypeStruct((8, tokens), jnp.float32)] * len(before)
+        return pl.pallas_call(
+            functools.partial(output_kernel, units, teams, ring, tokens, not before),
+            compiler_params=granted(10),
+            grid_spec=pltpu.PrefetchScalarGridSpec(
+                num_scalar_prefetch=1,
+                grid=(1,),
+                in_specs=in_vmem(len(units) + 1 + len(before)),
+                out_specs=in_vmem(len(shapes)),
+            ),
+            out_shape=shapes,
+        )(pos, *[pieces[unit] for unit in units], w_out, *before)
+
+    projected, squares = output(late, output(early, []))
     bit = 1
     while bit < shards:
         squares = squares + swap(squares, bit)

time: 120 us -> 112 us (0.933)
  waiting for transfers between devices: 47.2 us -> 35.4 us
  starting transfers between devices: 41.5 us -> 44.9 us
  Pallas kernels: 15.5 us -> 18 us
  local copies, waits for them, and re-layouts: 12.2 us -> 9.99 us
    ppermute x39 -> x33, waiting for transfers between devices: 47.2 us -> 16.6 us  [swap(): return lax.ppermute(x, 'psg', [(i, i ^ k) for i in range(shards)])]
    ppermute x0 -> x15, starting transfers between devices: none -> 25.9 us  [exchanged(): moved.append(lax.ppermute(part, 'psg', pairs))]
    ppermute x39 -> x33, starting transfers between devices: 41.5 us -> 19 us  [swap(): return lax.ppermute(x, 'psg', [(i, i ^ k) for i in range(shards)])]
    ppermute x0 -> x15, waiting for transfers between devices: none -> 18.8 us  [exchanged(): moved.append(lax.ppermute(part, 'psg', pairs))]
    pallas_call x5 -> x6, Pallas kernels: 10.7 us -> 13.3 us  [the longest x1 5.29 us: split_device(): pl.pallas_call(functools.partial(query_kernel, ring, heads), name='qp', c...]
    unnamed x39 -> x37, local copies, waits for them, and re-layouts: 9.34 us -> 7.11 us
  transfers between devices with their start and end apart: 39 -> 48, of which waited for: 17 -> 18; matrix products, arithmetic and copies ran while one was open for 4% -> 5% of each run, Pallas kernels for 10% -> 13%
where the time goes in v1:
time: 112 us; the launch traced here: 111 us
  starting transfers between devices  44.9 us (40%)
  waiting for transfers between devices  35.4 us (32%)
  Pallas kernels  18 us (16%)
  local copies, waits for them, and re-layouts  9.99 us (9%)
  other arithmetic  2.54 us (2%)
    ppermute x15, starting transfers between devices, exchanged(): moved.append(lax.ppermute(part, 'psg', pairs))  25.9 us
    ppermute x33, starting transfers between devices, swap(): return lax.ppermute(x, 'psg', [(i, i ^ k) for i in range(shards)])  19 us
    ppermute x15, waiting for transfers between devices, exchanged(): moved.append(lax.ppermute(part, 'psg', pairs))  18.8 us
    ppermute x33, waiting for transfers between devices, swap(): return lax.ppermute(x, 'psg', [(i, i ^ k) for i in range(shards)])  16.6 us
    unnamed x37, local copies, waits for them, and re-layouts  7.11 us
    pallas_call x1, Pallas kernels, split_device(): pl.pallas_call(functools.partial(query_kernel, ring, heads), name='qp', c...  5.29 us
    pallas_call x1, Pallas kernels, split_device(): pl.pallas_call(functools.partial(key_kernel, teams, ring), name='kp', com...  2.86 us
    pallas_call x1, Pallas kernels, split_device(): pl.pallas_call(functools.partial(value_kernel, teams, ring), name='vp', c...  2.62 us
  transfers between devices with their start and end apart: 48, of which 18 were waited for; matrix products, arithmetic and copies ran while one was open for 5% of the time, Pallas kernels for 13%

profile of v1, /device:TPU:0, one launch (start us, length us, event | category | flops | bytes accessed | tf_op | source)
XLA Modules:
  0.0 111.2 jit_solution(10119415871947202106)
XLA Ops:
  0.0 3.0 %collective-permute-start.9 = (bf16[128,512]{1,0:T(8,128)(2,1)}, bf16[128,512]{1,0:T(8,128)(2,1)}, u32[]{:S(2)}, u32[]{:S(2)}) collective-permute-start(bf16[128,512]{1,0:T(8,128)(2,1)} %refs_4_.1), channel_id=1, source_target_pairs={{0,2},{1,3},{2,0},{3,1},{4,6},{5,7},{6,4},{7,5},{8,10},{9,11},{10,... | collective-permute-start | bytes 393224 | tf_op jit(solution)/shard_map/ppermute | solution.py:398
  3.1 2.1 %constant_dynamic-slice_fusion = (bf16[64,2048]{1,0:T(8,128)(2,1)}, bf16[64,2048]{1,0:T(8,128)(2,1)}, bf16[64,2048]{1,0:T(8,128)(2,1)S(1)}, bf16[64,2048]{1,0:T(8,128)(2,1)}) fusion(bf16[64,8192]{1,0:T(8,128)(2,1)} %param.12, s32[]{:T(128)S(6)} %select_n.28, s32[]{:T(128)S(6)} %select_n.26, s32[]{:T(128)S(6)} %select_n.25, s32[]{:T(128)S(6)} %select_n.27), kind=kLoop, calls=%fused_computation.12 | loop fusion | bytes 2097168 | tf_op jit(solution)/shard_map/dynamic_slice | solution.py:416
  5.2 1.6 %collective-permute-start.5 = (bf16[64,2048]{1,0:T(8,128)(2,1)}, bf16[64,2048]{1,0:T(8,128)(2,1)}, u32[]{:S(2)}, u32[]{:S(2)}) collective-permute-start(bf16[64,2048]{1,0:T(8,128)(2,1)} %get-tuple-element.42), channel_id=1, source_target_pairs={{0,4},{1,5},{2,6},{3,7},{4,8},{5,9},{6,10},{7,11},{8,12},{9,13},{1... | collective-permute-start | bytes 786440 | tf_op jit(solution)/shard_map/ppermute | solution.py:412
  7.3 1.5 %collective-permute-start.21 = (bf16[512,512]{1,0:T(8,128)(2,1)}, bf16[512,512]{1,0:T(8,128)(2,1)S(1)}, u32[]{:S(2)}, u32[]{:S(2)}) collective-permute-start(bf16[512,512]{1,0:T(8,128)(2,1)} %refs_0_.1), channel_id=1, source_target_pairs={{0,2},{1,3},{2,0},{3,1},{4,6},{5,7},{6,4},{7,5},{8,10},{9,11},{10,... | collective-permute-start | bytes 1572872 | tf_op jit(solution)/shard_map/ppermute | solution.py:398
  9.8 5.3 %qp.1 = (f32[2,4,256,128]{3,2,1,0:T(8,128)S(1)}, f32[2,4,256,128]{3,2,1,0:T(8,128)}) custom-call(s32[2]{0:T(128)S(1)} %pad_add_fusion.pos, bf16[128,512]{1,0:T(8,128)(2,1)S(1)} %copy-done.1, bf16[512,4096]{1,0:T(8,128)(2,1)} %w_ref.1), custom_call_target="tpu_custom_call" | custom-call | flops 536870912 | bytes 4194304 | tf_op jit(solution)/shard_map/qp/pallas_call | solution.py:429
  15.1 2.7 %collective-permute-start.6 = (bf16[64,2048]{1,0:T(8,128)(2,1)S(1)}, bf16[64,2048]{1,0:T(8,128)(2,1)S(1)}, u32[]{:S(2)}, u32[]{:S(2)}) collective-permute-start(bf16[64,2048]{1,0:T(8,128)(2,1)S(1)} %copy-done.15), channel_id=1, source_target_pairs={{0,8},{1,9},{2,10},{3,11},{4,12},{5,13},{6,14},{7,15},{8,0},{9,1},... | collective-permute-start | bytes 786440 | tf_op jit(solution)/shard_map/ppermute | solution.py:412
  17.7 1.3 %collective-permute-start.7 = (bf16[64,2048]{1,0:T(8,128)(2,1)S(1)}, bf16[64,2048]{1,0:T(8,128)(2,1)S(1)}, u32[]{:S(2)}, u32[]{:S(2)}) collective-permute-start(bf16[64,2048]{1,0:T(8,128)(2,1)S(1)} %copy-done.14), channel_id=1, source_target_pairs={{0,12},{1,13},{2,14},{3,15},{4,0},{5,1},{6,2},{7,3},{8,4},{9,5},{1... | collective-permute-start | bytes 786440 | tf_op jit(solution)/shard_map/ppermute | solution.py:412
  19.1 11.8 %collective-permute-done.6.refs_2_ = bf16[64,2048]{1,0:T(8,128)(2,1)S(1)} collective-permute-done((bf16[64,2048]{1,0:T(8,128)(2,1)S(1)}, bf16[64,2048]{1,0:T(8,128)(2,1)S(1)}, u32[]{:S(2)}, u32[]{:S(2)}) %collective-permute-start.6) | collective-permute-done | bytes 262176 | tf_op jit(solution)/shard_map/ppermute | solution.py:412
  36.4 2.3 %tab.1 = (f32[800,128]{1,0:T(8,128)S(1)}, f32[800,128]{1,0:T(8,128)S(1)}, f32[128,128]{1,0:T(8,128)S(1)}, f32[128,128]{1,0:T(8,128)S(1)}) custom-call(s32[2]{0:T(128)S(1)} %pad_add_fusion.pos, s32[2]{0:T(128)S(1)} %copy-done.11, s32[2]{0:T(128)S(1)} %copy-done.12, s32[6]{0:T(128)S(1)} %reshape.28.orders, f32[1,128]{1,0:T(1,128)S(1)} %copy-done.13), custom_call_target="tpu_custom_call" | custom-call | flops 10240000 | bytes 819200 | tf_op jit(solution)/shard_map/tab/pallas_call | solution.py:465
  41.5 2.9 %kp.1 = (f32[288,128]{1,0:T(8,128)S(1)}, f32[288,128]{1,0:T(8,128)S(1)}, f32[288,128]{1,0:T(8,128)S(1)}, f32[288,128]{1,0:T(8,128)S(1)}, bf16[288,2048]{1,0:T(8,128)(2,1)S(1)}) custom-call(s32[2]{0:T(128)S(1)} %pad_add_fusion.pos, bf16[64,2048]{1,0:T(8,128)(2,1)S(1)} %get-tuple-element.43.refs_0_, bf16[64,2048]{1,0:T(8,128)(2,1)} %collective-permute-done.5.refs_1_, ...), custom_call_target="tpu_custom_call" | custom-call | flops 603979776 | bytes 3276800 | tf_op jit(solution)/shard_map/kp/pallas_call | solution.py:489
  44.4 2.6 %vp.1 = (f32[288,128]{1,0:T(8,128)S(1)}, bf16[288,128]{1,0:T(8,128)(2,1)S(1)}, bf16[288,128]{1,0:T(8,128)(2,1)S(1)}, bf16[288,128]{1,0:T(8,128)(2,1)S(1)}) custom-call(s32[2]{0:T(128)S(1)} %pad_add_fusion.pos, bf16[288,2048]{1,0:T(8,128)(2,1)S(1)} %get-tuple-element.32.rows_ref, bf16[512,512]{1,0:T(8,128)(2,1)S(1)} %copy-done.4, ...), custom_call_target="tpu_custom_call" | custom-call | flops 603979776 | bytes 3276800 | tf_op jit(solution)/shard_map/vp/pallas_call | solution.py:504
  47.0 4.7 %collective-permute-start.23 = (bf16[288,128]{1,0:T(8,128)(2,1)S(1)}, bf16[288,128]{1,0:T(8,128)(2,1)S(1)}, u32[]{:S(2)}, u32[]{:S(2)}) collective-permute-start(bf16[288,128]{1,0:T(8,128)(2,1)S(1)} %get-tuple-element.34), channel_id=1, source_target_pairs={{0,4},{1,5},{2,6},{3,7},{4,8},{5,9},{6,10},{7,11},{8,12},{9,13},{1... | collective-permute-start | bytes 221192 | tf_op jit(solution)/shard_map/ppermute | solution.py:412
  51.7 3.2 %collective-permute-start.24 = (bf16[288,128]{1,0:T(8,128)(2,1)S(1)}, bf16[288,128]{1,0:T(8,128)(2,1)S(1)}, u32[]{:S(2)}, u32[]{:S(2)}) collective-permute-start(bf16[288,128]{1,0:T(8,128)(2,1)S(1)} %get-tuple-element.35), channel_id=1, source_target_pairs={{0,8},{1,9},{2,10},{3,11},{4,12},{5,13},{6,14},{7,15},{8,0},{9,1},... | collective-permute-start | bytes 221192 | tf_op jit(solution)/shard_map/ppermute | solution.py:412
  55.0 2.1 %collective-permute-start.14 = (f16[288,128]{1,0:T(8,128)(2,1)S(1)}, f16[288,128]{1,0:T(8,128)(2,1)S(1)}, u32[]{:S(2)}, u32[]{:S(2)}) collective-permute-start(f16[288,128]{1,0:T(8,128)(2,1)S(1)} %convert_element_type.65), channel_id=1, source_target_pairs={{0,4},{1,5},{2,6},{3,7},{4,8},{5,9},{6,10},{7,11},{8,12},{9,13},{1... | collective-permute-start | bytes 221192 | tf_op jit(solution)/shard_map/ppermute | solution.py:412
  57.2 1.4 %add.83 = f32[2,4,256,128]{3,2,1,0:T(8,128)S(1)} add(f32[2,4,256,128]{3,2,1,0:T(8,128)S(1)} %get-tuple-element.22, f32[2,4,256,128]{3,2,1,0:T(8,128)} %collective-permute-done) | non-fusion elementwise | flops 262144 | bytes 3145728 | tf_op jit(solution)/shard_map/add | solution.py:453
  58.7 2.5 %collective-permute-start.16 = (f16[288,128]{1,0:T(8,128)(2,1)S(1)}, f16[288,128]{1,0:T(8,128)(2,1)S(1)}, u32[]{:S(2)}, u32[]{:S(2)}) collective-permute-start(f16[288,128]{1,0:T(8,128)(2,1)S(1)} %convert_element_type.69), channel_id=1, source_target_pairs={{0,12},{1,13},{2,14},{3,15},{4,0},{5,1},{6,2},{7,3},{8,4},{9,5},{1... | collective-permute-start | bytes 221192 | tf_op jit(solution)/shard_map/ppermute | solution.py:412
  61.1 1.8 %collective-permute-done.24 = bf16[288,128]{1,0:T(8,128)(2,1)S(1)} collective-permute-done((bf16[288,128]{1,0:T(8,128)(2,1)S(1)}, bf16[288,128]{1,0:T(8,128)(2,1)S(1)}, u32[]{:S(2)}, u32[]{:S(2)}) %collective-permute-start.24) | collective-permute-done | bytes 73760 | tf_op jit(solution)/shard_map/ppermute | solution.py:412
  63.4 1.7 %collective-permute-start.27 = (bf16[288,128]{1,0:T(8,128)(2,1)S(1)}, bf16[288,128]{1,0:T(8,128)(2,1)S(1)}, u32[]{:S(2)}, u32[]{:S(2)}) collective-permute-start(bf16[288,128]{1,0:T(8,128)(2,1)S(1)} %add_convert_fusion.refs_4_), channel_id=1, source_target_pairs={{0,2},{1,3},{2,0},{3,1},{4,6},{5,7},{6,4},{7,5},{8,10},{9,11},{10,... | collective-permute-start | bytes 221192 | tf_op jit(solution)/shard_map/ppermute | solution.py:398
  65.1 1.5 %collective-permute-done.15 = f16[288,128]{1,0:T(8,128)(2,1)S(1)} collective-permute-done((f16[288,128]{1,0:T(8,128)(2,1)S(1)}, f16[288,128]{1,0:T(8,128)(2,1)S(1)}, u32[]{:S(2)}, u32[]{:S(2)}) %collective-permute-start.15) | collective-permute-done | bytes 73760 | tf_op jit(solution)/shard_map/ppermute | solution.py:412
  67.2 2.7 %collective-permute-done.1 = f16[1,4,256,128]{3,2,1,0:T(8,128)(2,1)S(1)} collective-permute-done((f16[1,4,256,128]{3,2,1,0:T(8,128)(2,1)S(1)}, f16[1,4,256,128]{3,2,1,0:T(8,128)(2,1)S(1)}, u32[]{:S(2)}, u32[]{:S(2)}) %collective-permute-start.1) | collective-permute-done | bytes 262176 | tf_op jit(solution)/shard_map/ppermute | solution.py:398
  71.3 2.6 %collective-permute-start.4 = (f16[256,128]{1,0:T(8,128)(2,1)S(1)}, f16[256,128]{1,0:T(8,128)(2,1)S(1)}, u32[]{:S(2)}, u32[]{:S(2)}) collective-permute-start(f16[256,128]{1,0:T(8,128)(2,1)S(1)} %get-tuple-element.46), channel_id=1, source_target_pairs={{0,12},{1,13},{2,14},{3,15},{4,0},{5,1},{6,2},{7,3},{8,4},{9,5},{1... | collective-permute-start | bytes 196616 | tf_op jit(solution)/shard_map/ppermute | solution.py:412
  74.9 1.3 %collective-permute-done.2 = f16[256,128]{1,0:T(8,128)(2,1)S(1)} collective-permute-done((f16[256,128]{1,0:T(8,128)(2,1)S(1)}, f16[256,128]{1,0:T(8,128)(2,1)S(1)}, u32[]{:S(2)}, u32[]{:S(2)}) %collective-permute-start.2) | collective-permute-done | bytes 65568 | tf_op jit(solution)/shard_map/ppermute | solution.py:412
  77.8 2.5 %attend.1.refs_0_ = bf16[256,128]{1,0:T(8,128)(2,1)S(1)} custom-call(s32[2]{0:T(128)S(1)} %pad_add_fusion.pos, f32[256,128]{1,0:T(8,128)S(1)} %fusion.2.q_ref, f32[128,128]{1,0:T(8,128)S(1)} %get-tuple-element.24.cos_ref, f32[128,128]{1,0:T(8,128)S(1)} %get-tuple-element.25.sin_ref, bf16[800,128]{1,0:T(8,128)(2,1)S(1)} %turn.1.refs_0_, ...), custom_call_target="tpu_custom_call" | custom-call | tf_op jit(solution)/shard_map/attend/pallas_call | solution.py:542
  81.5 2.7 %collective-permute-start.33 = (bf16[256,128]{1,0:T(8,128)(2,1)S(1)}, bf16[256,128]{1,0:T(8,128)(2,1)S(1)}, u32[]{:S(2)}, u32[]{:S(2)}) collective-permute-start(bf16[256,128]{1,0:T(8,128)(2,1)S(1)} %attend.1.refs_0_), channel_id=1, source_target_pairs={{0,12},{1,13},{2,14},{3,15},{4,0},{5,1},{6,2},{7,3},{8,4},{9,5},{1... | collective-permute-start | bytes 196616 | tf_op jit(solution)/shard_map/ppermute | solution.py:412
  84.2 1.8 %collective-permute-start.34 = (bf16[256,128]{1,0:T(8,128)(2,1)S(1)}, bf16[256,128]{1,0:T(8,128)(2,1)S(1)}, u32[]{:S(2)}, u32[]{:S(2)}) collective-permute-start(bf16[256,128]{1,0:T(8,128)(2,1)S(1)} %attend.1.refs_0_), channel_id=1, source_target_pairs={{0,2},{1,3},{2,0},{3,1},{4,6},{5,7},{6,4},{7,5},{8,10},{9,11},{10,... | collective-permute-start | bytes 196616 | tf_op jit(solution)/shard_map/ppermute | solution.py:398
  87.1 1.8 %collective-permute-start.35 = (bf16[256,128]{1,0:T(8,128)(2,1)S(1)}, bf16[256,128]{1,0:T(8,128)(2,1)S(1)}, u32[]{:S(2)}, u32[]{:S(2)}) collective-permute-start(bf16[256,128]{1,0:T(8,128)(2,1)S(1)} %collective-permute-done.32.refs_1_), channel_id=1, source_target_pairs={{0,2},{1,3},{2,0},{3,1},{4,6},{5,7},{6,4},{7,5},{8,10},{9,11},{10,... | collective-permute-start | bytes 196616 | tf_op jit(solution)/shard_map/ppermute | solution.py:398
  90.7 1.5 %collective-permute-start.30 = (bf16[256,128]{1,0:T(8,128)(2,1)S(1)}, bf16[256,128]{1,0:T(8,128)(2,1)S(1)}, u32[]{:S(2)}, u32[]{:S(2)}) collective-permute-start(bf16[256,128]{1,0:T(8,128)(2,1)S(1)} %collective-permute-done.29.refs_2_), channel_id=1, source_target_pairs={{0,2},{1,3},{2,0},{3,1},{4,6},{5,7},{6,4},{7,5},{8,10},{9,11},{10,... | collective-permute-start | bytes 196616 | tf_op jit(solution)/shard_map/ppermute | solution.py:398
  98.7 1.5 %collective-permute-start.45 = (f32[8,128]{1,0:T(8,128)S(1)}, f32[8,128]{1,0:T(8,128)S(1)}, u32[]{:S(2)}, u32[]{:S(2)}) collective-permute-start(f32[8,128]{1,0:T(8,128)S(1)} %add.101), channel_id=1, source_target_pairs={{0,2},{1,3},{2,0},{3,1},{4,6},{5,7},{6,4},{7,5},{8,10},{9,11},{10,... | collective-permute-start | bytes 12296 | tf_op jit(solution)/shard_map/ppermute | solution.py:398
  100.2 2.1 %collective-permute-done.45 = f32[8,128]{1,0:T(8,128)S(1)} collective-permute-done((f32[8,128]{1,0:T(8,128)S(1)}, f32[8,128]{1,0:T(8,128)S(1)}, u32[]{:S(2)}, u32[]{:S(2)}) %collective-permute-start.45) | collective-permute-done | bytes 4128 | tf_op jit(solution)/shard_map/ppermute | solution.py:398
  102.3 3.6 %collective-permute-done.46 = f32[8,128]{1,0:T(8,128)S(1)} collective-permute-done((f32[8,128]{1,0:T(8,128)S(1)}, f32[8,128]{1,0:T(8,128)S(1)}, u32[]{:S(2)}, u32[]{:S(2)}) %collective-permute-start.46) | collective-permute-done | bytes 4128 | tf_op jit(solution)/shard_map/ppermute | solution.py:398
  105.9 1.5 %collective-permute-start.47 = (f32[8,128]{1,0:T(8,128)S(1)}, f32[8,128]{1,0:T(8,128)S(1)}, u32[]{:S(2)}, u32[]{:S(2)}) collective-permute-start(f32[8,128]{1,0:T(8,128)S(1)} %add.103), channel_id=1, source_target_pairs={{0,8},{1,9},{2,10},{3,11},{4,12},{5,13},{6,14},{7,15},{8,0},{9,1},... | collective-permute-start | bytes 12296 | tf_op jit(solution)/shard_map/ppermute | solution.py:398
  107.4 3.0 %collective-permute-done.47 = f32[8,128]{1,0:T(8,128)S(1)} collective-permute-done((f32[8,128]{1,0:T(8,128)S(1)}, f32[8,128]{1,0:T(8,128)S(1)}, u32[]{:S(2)}, u32[]{:S(2)}) %collective-permute-start.47) | collective-permute-done | bytes 4128 | tf_op jit(solution)/shard_map/ppermute | solution.py:398
  (128 shorter events, 26.3 us)
Async XLA Ops:
  0.0 15.0 %collective-permute-start.9 = (bf16[128,512]{1,0:T(8,128)(2,1)}, bf16[128,512]{1,0:T(8,128)(2,1)}, u32[]{:S(2)}, u32[]{:S(2)}) collective-permute-start(bf16[128,512]{1,0:T(8,128)(2,1)} %refs_4_.1), channel_id=1, source_target_pairs={{0,2},{1,3},{2,0},{3,1},{4,6},{5,7},{6,4},{7,5},{8,10},{9,11},{10,... | collective-permute-start | bytes 393224 | tf_op jit(solution)/shard_map/ppermute | solution.py:398
  3.1 12.0 %collective-permute-start.8 = (bf16[128,512]{1,0:T(8,128)(2,1)}, bf16[128,512]{1,0:T(8,128)(2,1)}, u32[]{:S(2)}, u32[]{:S(2)}) collective-permute-start(bf16[128,512]{1,0:T(8,128)(2,1)} %refs_4_.1), channel_id=1, source_target_pairs={{0,1},{1,0},{2,3},{3,2},{4,5},{5,4},{6,7},{7,6},{8,9},{9,8},{10,11... | collective-permute-start | bytes 393224 | tf_op jit(solution)/shard_map/ppermute | solution.py:398
  5.2 12.6 %collective-permute-start.5 = (bf16[64,2048]{1,0:T(8,128)(2,1)}, bf16[64,2048]{1,0:T(8,128)(2,1)}, u32[]{:S(2)}, u32[]{:S(2)}) collective-permute-start(bf16[64,2048]{1,0:T(8,128)(2,1)} %get-tuple-element.42), channel_id=1, source_target_pairs={{0,4},{1,5},{2,6},{3,7},{4,8},{5,9},{6,10},{7,11},{8,12},{9,13},{1... | collective-permute-start | bytes 786440 | tf_op jit(solution)/shard_map/ppermute | solution.py:412
  6.7 26.1 %collective-permute-start.12 = (bf16[512,512]{1,0:T(8,128)(2,1)}, bf16[512,512]{1,0:T(8,128)(2,1)S(1)}, u32[]{:S(2)}, u32[]{:S(2)}) collective-permute-start(bf16[512,512]{1,0:T(8,128)(2,1)} %refs_8_.1), channel_id=1, source_target_pairs={{0,2},{1,3},{2,0},{3,1},{4,6},{5,7},{6,4},{7,5},{8,10},{9,11},{10,... | collective-permute-start | bytes 1572872 | tf_op jit(solution)/shard_map/ppermute | solution.py:398
  7.3 26.7 %collective-permute-start.21 = (bf16[512,512]{1,0:T(8,128)(2,1)}, bf16[512,512]{1,0:T(8,128)(2,1)S(1)}, u32[]{:S(2)}, u32[]{:S(2)}) collective-permute-start(bf16[512,512]{1,0:T(8,128)(2,1)} %refs_0_.1), channel_id=1, source_target_pairs={{0,2},{1,3},{2,0},{3,1},{4,6},{5,7},{6,4},{7,5},{8,10},{9,11},{10,... | collective-permute-start | bytes 1572872 | tf_op jit(solution)/shard_map/ppermute | solution.py:398
  15.0 42.0 %collective-permute-start = (f32[2,4,256,128]{3,2,1,0:T(8,128)}, f32[2,4,256,128]{3,2,1,0:T(8,128)}, u32[]{:S(2)}, u32[]{:S(2)}) collective-permute-start(f32[2,4,256,128]{3,2,1,0:T(8,128)} %get-tuple-element.23), channel_id=1, source_target_pairs={{0,1},{1,0},{2,3},{3,2},{4,5},{5,4},{6,7},{7,6},{8,9},{9,8},{10,11... | collective-permute-start | bytes 3145736 | tf_op jit(solution)/shard_map/ppermute | solution.py:398
  15.1 15.8 %collective-permute-start.6 = (bf16[64,2048]{1,0:T(8,128)(2,1)S(1)}, bf16[64,2048]{1,0:T(8,128)(2,1)S(1)}, u32[]{:S(2)}, u32[]{:S(2)}) collective-permute-start(bf16[64,2048]{1,0:T(8,128)(2,1)S(1)} %copy-done.15), channel_id=1, source_target_pairs={{0,8},{1,9},{2,10},{3,11},{4,12},{5,13},{6,14},{7,15},{8,0},{9,1},... | collective-permute-start | bytes 786440 | tf_op jit(solution)/shard_map/ppermute | solution.py:412
  17.7 13.9 %collective-permute-start.7 = (bf16[64,2048]{1,0:T(8,128)(2,1)S(1)}, bf16[64,2048]{1,0:T(8,128)(2,1)S(1)}, u32[]{:S(2)}, u32[]{:S(2)}) collective-permute-start(bf16[64,2048]{1,0:T(8,128)(2,1)S(1)} %copy-done.14), channel_id=1, source_target_pairs={{0,12},{1,13},{2,14},{3,15},{4,0},{5,1},{6,2},{7,3},{8,4},{9,5},{1... | collective-permute-start | bytes 786440 | tf_op jit(solution)/shard_map/ppermute | solution.py:412
  32.3 6.4 %collective-permute-start.11 = (bf16[512,512]{1,0:T(8,128)(2,1)S(1)}, bf16[512,512]{1,0:T(8,128)(2,1)}, u32[]{:S(2)}, u32[]{:S(2)}) collective-permute-start(bf16[512,512]{1,0:T(8,128)(2,1)S(1)} %copy-done.3), channel_id=1, source_target_pairs={{0,1},{1,0},{2,3},{3,2},{4,5},{5,4},{6,7},{7,6},{8,9},{9,8},{10,11... | collective-permute-start | bytes 1572872 | tf_op jit(solution)/shard_map/ppermute | solution.py:398
  32.8 5.9 %collective-permute-start.13 = (bf16[512,512]{1,0:T(8,128)(2,1)S(1)}, bf16[512,512]{1,0:T(8,128)(2,1)}, u32[]{:S(2)}, u32[]{:S(2)}) collective-permute-start(bf16[512,512]{1,0:T(8,128)(2,1)S(1)} %collective-permute-done.12.refs_10_), channel_id=1, source_target_pairs={{0,1},{1,0},{2,3},{3,2},{4,5},{5,4},{6,7},{7,6},{8,9},{9,8},{10,11... | collective-permute-start | bytes 1572872 | tf_op jit(solution)/shard_map/ppermute | solution.py:398
  33.8 10.6 %collective-permute-start.20 = (bf16[512,512]{1,0:T(8,128)(2,1)S(1)}, bf16[512,512]{1,0:T(8,128)(2,1)}, u32[]{:S(2)}, u32[]{:S(2)}) collective-permute-start(bf16[512,512]{1,0:T(8,128)(2,1)S(1)} %copy-done.4), channel_id=1, source_target_pairs={{0,1},{1,0},{2,3},{3,2},{4,5},{5,4},{6,7},{7,6},{8,9},{9,8},{10,11... | collective-permute-start | bytes 1572872 | tf_op jit(solution)/shard_map/ppermute | solution.py:398
  34.0 10.4 %collective-permute-start.22 = (bf16[512,512]{1,0:T(8,128)(2,1)S(1)}, bf16[512,512]{1,0:T(8,128)(2,1)}, u32[]{:S(2)}, u32[]{:S(2)}) collective-permute-start(bf16[512,512]{1,0:T(8,128)(2,1)S(1)} %collective-permute-done.21.refs_2_), channel_id=1, source_target_pairs={{0,1},{1,0},{2,3},{3,2},{4,5},{5,4},{6,7},{7,6},{8,9},{9,8},{10,11... | collective-permute-start | bytes 1572872 | tf_op jit(solution)/shard_map/ppermute | solution.py:398
  47.0 11.6 %collective-permute-start.23 = (bf16[288,128]{1,0:T(8,128)(2,1)S(1)}, bf16[288,128]{1,0:T(8,128)(2,1)S(1)}, u32[]{:S(2)}, u32[]{:S(2)}) collective-permute-start(bf16[288,128]{1,0:T(8,128)(2,1)S(1)} %get-tuple-element.34), channel_id=1, source_target_pairs={{0,4},{1,5},{2,6},{3,7},{4,8},{5,9},{6,10},{7,11},{8,12},{9,13},{1... | collective-permute-start | bytes 221192 | tf_op jit(solution)/shard_map/ppermute | solution.py:412
  51.7 11.2 %collective-permute-start.24 = (bf16[288,128]{1,0:T(8,128)(2,1)S(1)}, bf16[288,128]{1,0:T(8,128)(2,1)S(1)}, u32[]{:S(2)}, u32[]{:S(2)}) collective-permute-start(bf16[288,128]{1,0:T(8,128)(2,1)S(1)} %get-tuple-element.35), channel_id=1, source_target_pairs={{0,8},{1,9},{2,10},{3,11},{4,12},{5,13},{6,14},{7,15},{8,0},{9,1},... | collective-permute-start | bytes 221192 | tf_op jit(solution)/shard_map/ppermute | solution.py:412
  55.0 8.3 %collective-permute-start.25 = (bf16[288,128]{1,0:T(8,128)(2,1)S(1)}, bf16[288,128]{1,0:T(8,128)(2,1)S(1)}, u32[]{:S(2)}, u32[]{:S(2)}) collective-permute-start(bf16[288,128]{1,0:T(8,128)(2,1)S(1)} %get-tuple-element.36), channel_id=1, source_target_pairs={{0,12},{1,13},{2,14},{3,15},{4,0},{5,1},{6,2},{7,3},{8,4},{9,5},{1... | collective-permute-start | bytes 221192 | tf_op jit(solution)/shard_map/ppermute | solution.py:412
  55.0 10.1 %collective-permute-start.14 = (f16[288,128]{1,0:T(8,128)(2,1)S(1)}, f16[288,128]{1,0:T(8,128)(2,1)S(1)}, u32[]{:S(2)}, u32[]{:S(2)}) collective-permute-start(f16[288,128]{1,0:T(8,128)(2,1)S(1)} %convert_element_type.65), channel_id=1, source_target_pairs={{0,4},{1,5},{2,6},{3,7},{4,8},{5,9},{6,10},{7,11},{8,12},{9,13},{1... | collective-permute-start | bytes 221192 | tf_op jit(solution)/shard_map/ppermute | solution.py:412
  57.1 9.5 %collective-permute-start.15 = (f16[288,128]{1,0:T(8,128)(2,1)S(1)}, f16[288,128]{1,0:T(8,128)(2,1)S(1)}, u32[]{:S(2)}, u32[]{:S(2)}) collective-permute-start(f16[288,128]{1,0:T(8,128)(2,1)S(1)} %convert_element_type.67), channel_id=1, source_target_pairs={{0,8},{1,9},{2,10},{3,11},{4,12},{5,13},{6,14},{7,15},{8,0},{9,1},... | collective-permute-start | bytes 221192 | tf_op jit(solution)/shard_map/ppermute | solution.py:412
  58.7 7.9 %collective-permute-start.16 = (f16[288,128]{1,0:T(8,128)(2,1)S(1)}, f16[288,128]{1,0:T(8,128)(2,1)S(1)}, u32[]{:S(2)}, u32[]{:S(2)}) collective-permute-start(f16[288,128]{1,0:T(8,128)(2,1)S(1)} %convert_element_type.69), channel_id=1, source_target_pairs={{0,12},{1,13},{2,14},{3,15},{4,0},{5,1},{6,2},{7,3},{8,4},{9,5},{1... | collective-permute-start | bytes 221192 | tf_op jit(solution)/shard_map/ppermute | solution.py:412
  63.0 7.0 %collective-permute-start.1 = (f16[1,4,256,128]{3,2,1,0:T(8,128)(2,1)S(1)}, f16[1,4,256,128]{3,2,1,0:T(8,128)(2,1)S(1)}, u32[]{:S(2)}, u32[]{:S(2)}) collective-permute-start(f16[1,4,256,128]{3,2,1,0:T(8,128)(2,1)S(1)} %slice_convert_fusion), channel_id=1, source_target_pairs={{0,2},{1,3},{2,0},{3,1},{4,6},{5,7},{6,4},{7,5},{8,10},{9,11},{10,... | collective-permute-start | bytes 786440 | tf_op jit(solution)/shard_map/ppermute | solution.py:398
  63.4 10.6 %collective-permute-start.27 = (bf16[288,128]{1,0:T(8,128)(2,1)S(1)}, bf16[288,128]{1,0:T(8,128)(2,1)S(1)}, u32[]{:S(2)}, u32[]{:S(2)}) collective-permute-start(bf16[288,128]{1,0:T(8,128)(2,1)S(1)} %add_convert_fusion.refs_4_), channel_id=1, source_target_pairs={{0,2},{1,3},{2,0},{3,1},{4,6},{5,7},{6,4},{7,5},{8,10},{9,11},{10,... | collective-permute-start | bytes 221192 | tf_op jit(solution)/shard_map/ppermute | solution.py:398
  66.8 8.1 %collective-permute-start.18 = (bf16[800,128]{1,0:T(8,128)(2,1)S(1)}, bf16[800,128]{1,0:T(8,128)(2,1)S(1)}, u32[]{:S(2)}, u32[]{:S(2)}) collective-permute-start(bf16[800,128]{1,0:T(8,128)(2,1)S(1)} %turn.1.refs_0_), channel_id=1, source_target_pairs={{0,2},{1,3},{2,0},{3,1},{4,6},{5,7},{6,4},{7,5},{8,10},{9,11},{10,... | collective-permute-start | bytes 614408 | tf_op jit(solution)/shard_map/ppermute | solution.py:398
  70.1 6.1 %collective-permute-start.2 = (f16[256,128]{1,0:T(8,128)(2,1)S(1)}, f16[256,128]{1,0:T(8,128)(2,1)S(1)}, u32[]{:S(2)}, u32[]{:S(2)}) collective-permute-start(f16[256,128]{1,0:T(8,128)(2,1)S(1)} %get-tuple-element.45), channel_id=1, source_target_pairs={{0,4},{1,5},{2,6},{3,7},{4,8},{5,9},{6,10},{7,11},{8,12},{9,13},{1... | collective-permute-start | bytes 196616 | tf_op jit(solution)/shard_map/ppermute | solution.py:412
  70.2 6.1 %collective-permute-start.3 = (f16[256,128]{1,0:T(8,128)(2,1)S(1)}, f16[256,128]{1,0:T(8,128)(2,1)S(1)}, u32[]{:S(2)}, u32[]{:S(2)}) collective-permute-start(f16[256,128]{1,0:T(8,128)(2,1)S(1)} %get-tuple-element.47), channel_id=1, source_target_pairs={{0,8},{1,9},{2,10},{3,11},{4,12},{5,13},{6,14},{7,15},{8,0},{9,1},... | collective-permute-start | bytes 196616 | tf_op jit(solution)/shard_map/ppermute | solution.py:412
  71.3 5.6 %collective-permute-start.4 = (f16[256,128]{1,0:T(8,128)(2,1)S(1)}, f16[256,128]{1,0:T(8,128)(2,1)S(1)}, u32[]{:S(2)}, u32[]{:S(2)}) collective-permute-start(f16[256,128]{1,0:T(8,128)(2,1)S(1)} %get-tuple-element.46), channel_id=1, source_target_pairs={{0,12},{1,13},{2,14},{3,15},{4,0},{5,1},{6,2},{7,3},{8,4},{9,5},{1... | collective-permute-start | bytes 196616 | tf_op jit(solution)/shard_map/ppermute | solution.py:412
  80.3 6.8 %collective-permute-start.32 = (bf16[256,128]{1,0:T(8,128)(2,1)S(1)}, bf16[256,128]{1,0:T(8,128)(2,1)S(1)}, u32[]{:S(2)}, u32[]{:S(2)}) collective-permute-start(bf16[256,128]{1,0:T(8,128)(2,1)S(1)} %attend.1.refs_0_), channel_id=1, source_target_pairs={{0,4},{1,5},{2,6},{3,7},{4,8},{5,9},{6,10},{7,11},{8,12},{9,13},{1... | collective-permute-start | bytes 196616 | tf_op jit(solution)/shard_map/ppermute | solution.py:412
  81.5 7.5 %collective-permute-start.33 = (bf16[256,128]{1,0:T(8,128)(2,1)S(1)}, bf16[256,128]{1,0:T(8,128)(2,1)S(1)}, u32[]{:S(2)}, u32[]{:S(2)}) collective-permute-start(bf16[256,128]{1,0:T(8,128)(2,1)S(1)} %attend.1.refs_0_), channel_id=1, source_target_pairs={{0,12},{1,13},{2,14},{3,15},{4,0},{5,1},{6,2},{7,3},{8,4},{9,5},{1... | collective-permute-start | bytes 196616 | tf_op jit(solution)/shard_map/ppermute | solution.py:412
  84.2 6.0 %collective-permute-start.29 = (bf16[256,128]{1,0:T(8,128)(2,1)S(1)}, bf16[256,128]{1,0:T(8,128)(2,1)S(1)}, u32[]{:S(2)}, u32[]{:S(2)}) collective-permute-start(bf16[256,128]{1,0:T(8,128)(2,1)S(1)} %attend.1.refs_0_), channel_id=1, source_target_pairs={{0,8},{1,9},{2,10},{3,11},{4,12},{5,13},{6,14},{7,15},{8,0},{9,1},... | collective-permute-start | bytes 196616 | tf_op jit(solution)/shard_map/ppermute | solution.py:412
  84.2 6.0 %collective-permute-start.34 = (bf16[256,128]{1,0:T(8,128)(2,1)S(1)}, bf16[256,128]{1,0:T(8,128)(2,1)S(1)}, u32[]{:S(2)}, u32[]{:S(2)}) collective-permute-start(bf16[256,128]{1,0:T(8,128)(2,1)S(1)} %attend.1.refs_0_), channel_id=1, source_target_pairs={{0,2},{1,3},{2,0},{3,1},{4,6},{5,7},{6,4},{7,5},{8,10},{9,11},{10,... | collective-permute-start | bytes 196616 | tf_op jit(solution)/shard_map/ppermute | solution.py:398
  86.0 4.7 %collective-permute-start.37 = (bf16[256,128]{1,0:T(8,128)(2,1)S(1)}, bf16[256,128]{1,0:T(8,128)(2,1)S(1)}, u32[]{:S(2)}, u32[]{:S(2)}) collective-permute-start(bf16[256,128]{1,0:T(8,128)(2,1)S(1)} %attend.1.refs_0_), channel_id=1, source_target_pairs={{0,1},{1,0},{2,3},{3,2},{4,5},{5,4},{6,7},{7,6},{8,9},{9,8},{10,11... | collective-permute-start | bytes 196616 | tf_op jit(solution)/shard_map/ppermute | solution.py:398
  87.1 5.1 %collective-permute-start.35 = (bf16[256,128]{1,0:T(8,128)(2,1)S(1)}, bf16[256,128]{1,0:T(8,128)(2,1)S(1)}, u32[]{:S(2)}, u32[]{:S(2)}) collective-permute-start(bf16[256,128]{1,0:T(8,128)(2,1)S(1)} %collective-permute-done.32.refs_1_), channel_id=1, source_target_pairs={{0,2},{1,3},{2,0},{3,1},{4,6},{5,7},{6,4},{7,5},{8,10},{9,11},{10,... | collective-permute-start | bytes 196616 | tf_op jit(solution)/shard_map/ppermute | solution.py:398
  88.9 4.3 %collective-permute-start.36 = (bf16[256,128]{1,0:T(8,128)(2,1)S(1)}, bf16[256,128]{1,0:T(8,128)(2,1)S(1)}, u32[]{:S(2)}, u32[]{:S(2)}) collective-permute-start(bf16[256,128]{1,0:T(8,128)(2,1)S(1)} %collective-permute-done.33.refs_3_), channel_id=1, source_target_pairs={{0,2},{1,3},{2,0},{3,1},{4,6},{5,7},{6,4},{7,5},{8,10},{9,11},{10,... | collective-permute-start | bytes 196616 | tf_op jit(solution)/shard_map/ppermute | solution.py:398
  105.9 4.5 %collective-permute-start.47 = (f32[8,128]{1,0:T(8,128)S(1)}, f32[8,128]{1,0:T(8,128)S(1)}, u32[]{:S(2)}, u32[]{:S(2)}) collective-permute-start(f32[8,128]{1,0:T(8,128)S(1)} %add.103), channel_id=1, source_target_pairs={{0,8},{1,9},{2,10},{3,11},{4,12},{5,13},{6,14},{7,15},{8,0},{9,1},... | collective-permute-start | bytes 12296 | tf_op jit(solution)/shard_map/ppermute | solution.py:398
  (34 other events, 335.2 us)

commit v2 on v1

--- a/solution.py
+++ b/solution.py
@@ -359,13 +359,12 @@
         refs[0][...] = total
         return
     refs[1][...] = total
-    refs[2][...] = lax.dot_general(
-        jnp.ones((8, total.shape[1]), jnp.float32),
-        total * total,
-        ROWS_COLUMNS,
-        precision=lax.Precision.HIGHEST,
-        preferred_element_type=jnp.float32,
-    )
+    squares = total * total
+    squares = sum(
+        squares[:, first : first + HEAD_SIZE] for first in range(0, total.shape[1], HEAD_SIZE)
+    )
+    sums = jnp.sum(jnp.transpose(squares), axis=0, keepdims=True)
+    refs[2][...] = jnp.broadcast_to(sums, refs[2].shape)
 
 
 def split_device(
@@ -429,7 +428,7 @@
     keep, send = pl.pallas_call(
         functools.partial(query_kernel, ring, heads),
         name="qp",
-        compiler_params=granted(10),
+        compiler_params=granted(6),
         grid_spec=pltpu.PrefetchScalarGridSpec(
             num_scalar_prefetch=1,
             grid=(teams,),
@@ -489,7 +488,7 @@
     *key_parts, all_rows = pl.pallas_call(
         functools.partial(key_kernel, teams, ring),
         name="kp",
-        compiler_params=granted(14),
+        compiler_params=granted(8),
         grid_spec=pltpu.PrefetchScalarGridSpec(
             num_scalar_prefetch=1,
             grid=(1,),
@@ -504,7 +503,7 @@
     value_parts = pl.pallas_call(
         functools.partial(value_kernel, teams, ring),
         name="vp",
-        compiler_params=granted(10),
+        compiler_params=granted(6),
         grid_spec=pltpu.PrefetchScalarGridSpec(
             num_scalar_prefetch=1,
             grid=(1,),
@@ -542,7 +541,7 @@
     attended = pl.pallas_call(
         functools.partial(attend_kernel, perms, ring, teams * rows, tokens),
         name="attend",
-        compiler_params=granted(14),
+        compiler_params=granted(8),
         grid_spec=pltpu.PrefetchScalarGridSpec(
             num_scalar_prefetch=1,
             grid=(1,),
@@ -568,7 +567,7 @@
         for (kb, ka), piece in list(pieces.items()):
             pieces[kb | bit, ka] = swap(piece, bit)
 
-    late = [(kb, ka) for kb, ka in pieces if ka == teams // 2 and kb & (ring // 2)]
+    late = [(kb, ka) for kb, ka in pieces if ka == teams // 2 or ka and kb & (ring // 2)]
     early = [unit for unit in pieces if unit not in late]
 
     def output(units, before):
@@ -576,7 +575,7 @@
         shapes = [projected_shape] + [jax.ShapeDtypeStruct((8, tokens), jnp.float32)] * len(before)
         return pl.pallas_call(
             functools.partial(output_kernel, units, teams, ring, tokens, not before),
-            compiler_params=granted(10),
+            compiler_params=granted(6),
             grid_spec=pltpu.PrefetchScalarGridSpec(
                 num_scalar_prefetch=1,
                 grid=(1,),

time: 112 us -> 113 us (level)
  waiting for transfers between devices: 35.4 us -> 37.2 us
    ppermute x33, waiting for transfers between devices: 16.6 us -> 18.5 us  [swap(): return lax.ppermute(x, 'psg', [(i, i ^ k) for i in range(shards)])]
  transfers between devices with their start and end apart: 48 -> 48, of which waited for: 18 -> 20; matrix products, arithmetic and copies ran while one was open for 5% -> 5% of each run, Pallas kernels for 13% -> 13%
where the time goes in v2:
time: 113 us; the launch traced here: 112 us
  starting transfers between devices  44.3 us (39%)
  waiting for transfers between devices  37.2 us (33%)
  Pallas kernels  17.8 us (16%)
  local copies, waits for them, and re-layouts  9.99 us (9%)
  other arithmetic  2.51 us (2%)
    ppermute x15, starting transfers between devices, exchanged(): moved.append(lax.ppermute(part, 'psg', pairs))  25.9 us
    ppermute x15, waiting for transfers between devices, exchanged(): moved.append(lax.ppermute(part, 'psg', pairs))  18.7 us
    ppermute x33, waiting for transfers between devices, swap(): return lax.ppermute(x, 'psg', [(i, i ^ k) for i in range(shards)])  18.5 us
    ppermute x33, starting transfers between devices, swap(): return lax.ppermute(x, 'psg', [(i, i ^ k) for i in range(shards)])  18.5 us
    unnamed x37, local copies, waits for them, and re-layouts  7.11 us
    pallas_call x1, Pallas kernels, split_device(): pl.pallas_call(functools.partial(query_kernel, ring, heads), name='qp', c...  5.29 us
    pallas_call x1, Pallas kernels, split_device(): pl.pallas_call(functools.partial(key_kernel, teams, ring), name='kp', com...  2.86 us
    pallas_call x1, Pallas kernels, split_device(): pl.pallas_call(functools.partial(value_kernel, teams, ring), name='vp', c...  2.62 us
  transfers between devices with their start and end apart: 48, of which 20 were waited for; matrix products, arithmetic and copies ran while one was open for 5% of the time, Pallas kernels for 13%

profile of v2, /device:TPU:0, one launch (start us, length us, event | category | flops | bytes accessed | tf_op | source)
XLA Modules:
  0.0 112.2 jit_solution(14521908859704827790)
XLA Ops:
  0.0 3.0 %collective-permute-start.9 = (bf16[128,512]{1,0:T(8,128)(2,1)}, bf16[128,512]{1,0:T(8,128)(2,1)}, u32[]{:S(2)}, u32[]{:S(2)}) collective-permute-start(bf16[128,512]{1,0:T(8,128)(2,1)} %refs_4_.1), channel_id=1, source_target_pairs={{0,2},{1,3},{2,0},{3,1},{4,6},{5,7},{6,4},{7,5},{8,10},{9,11},{10,... | collective-permute-start | bytes 393224 | tf_op jit(solution)/shard_map/ppermute | solution.py:397
  3.1 2.1 %constant_dynamic-slice_fusion = (bf16[64,2048]{1,0:T(8,128)(2,1)}, bf16[64,2048]{1,0:T(8,128)(2,1)}, bf16[64,2048]{1,0:T(8,128)(2,1)S(1)}, bf16[64,2048]{1,0:T(8,128)(2,1)}) fusion(bf16[64,8192]{1,0:T(8,128)(2,1)} %param.12, s32[]{:T(128)S(6)} %select_n.28, s32[]{:T(128)S(6)} %select_n.26, s32[]{:T(128)S(6)} %select_n.25, s32[]{:T(128)S(6)} %select_n.27), kind=kLoop, calls=%fused_computation.12 | loop fusion | bytes 2097168 | tf_op jit(solution)/shard_map/dynamic_slice | solution.py:415
  5.2 1.6 %collective-permute-start.5 = (bf16[64,2048]{1,0:T(8,128)(2,1)}, bf16[64,2048]{1,0:T(8,128)(2,1)}, u32[]{:S(2)}, u32[]{:S(2)}) collective-permute-start(bf16[64,2048]{1,0:T(8,128)(2,1)} %get-tuple-element.42), channel_id=1, source_target_pairs={{0,4},{1,5},{2,6},{3,7},{4,8},{5,9},{6,10},{7,11},{8,12},{9,13},{1... | collective-permute-start | bytes 786440 | tf_op jit(solution)/shard_map/ppermute | solution.py:411
  7.3 1.5 %collective-permute-start.21 = (bf16[512,512]{1,0:T(8,128)(2,1)}, bf16[512,512]{1,0:T(8,128)(2,1)S(1)}, u32[]{:S(2)}, u32[]{:S(2)}) collective-permute-start(bf16[512,512]{1,0:T(8,128)(2,1)} %refs_0_.1), channel_id=1, source_target_pairs={{0,2},{1,3},{2,0},{3,1},{4,6},{5,7},{6,4},{7,5},{8,10},{9,11},{10,... | collective-permute-start | bytes 1572872 | tf_op jit(solution)/shard_map/ppermute | solution.py:397
  9.8 5.3 %qp.1 = (f32[2,4,256,128]{3,2,1,0:T(8,128)S(1)}, f32[2,4,256,128]{3,2,1,0:T(8,128)}) custom-call(s32[2]{0:T(128)S(1)} %pad_add_fusion.pos, bf16[128,512]{1,0:T(8,128)(2,1)S(1)} %copy-done.1, bf16[512,4096]{1,0:T(8,128)(2,1)} %w_ref.1), custom_call_target="tpu_custom_call" | custom-call | flops 536870912 | bytes 4194304 | tf_op jit(solution)/shard_map/qp/pallas_call | solution.py:428
  15.1 2.7 %collective-permute-start.6 = (bf16[64,2048]{1,0:T(8,128)(2,1)S(1)}, bf16[64,2048]{1,0:T(8,128)(2,1)S(1)}, u32[]{:S(2)}, u32[]{:S(2)}) collective-permute-start(bf16[64,2048]{1,0:T(8,128)(2,1)S(1)} %copy-done.15), channel_id=1, source_target_pairs={{0,8},{1,9},{2,10},{3,11},{4,12},{5,13},{6,14},{7,15},{8,0},{9,1},... | collective-permute-start | bytes 786440 | tf_op jit(solution)/shard_map/ppermute | solution.py:411
  17.7 1.3 %collective-permute-start.7 = (bf16[64,2048]{1,0:T(8,128)(2,1)S(1)}, bf16[64,2048]{1,0:T(8,128)(2,1)S(1)}, u32[]{:S(2)}, u32[]{:S(2)}) collective-permute-start(bf16[64,2048]{1,0:T(8,128)(2,1)S(1)} %copy-done.14), channel_id=1, source_target_pairs={{0,12},{1,13},{2,14},{3,15},{4,0},{5,1},{6,2},{7,3},{8,4},{9,5},{1... | collective-permute-start | bytes 786440 | tf_op jit(solution)/shard_map/ppermute | solution.py:411
  19.1 11.8 %collective-permute-done.6.refs_2_ = bf16[64,2048]{1,0:T(8,128)(2,1)S(1)} collective-permute-done((bf16[64,2048]{1,0:T(8,128)(2,1)S(1)}, bf16[64,2048]{1,0:T(8,128)(2,1)S(1)}, u32[]{:S(2)}, u32[]{:S(2)}) %collective-permute-start.6) | collective-permute-done | bytes 262176 | tf_op jit(solution)/shard_map/ppermute | solution.py:411
  36.4 2.3 %tab.1 = (f32[800,128]{1,0:T(8,128)S(1)}, f32[800,128]{1,0:T(8,128)S(1)}, f32[128,128]{1,0:T(8,128)S(1)}, f32[128,128]{1,0:T(8,128)S(1)}) custom-call(s32[2]{0:T(128)S(1)} %pad_add_fusion.pos, s32[2]{0:T(128)S(1)} %copy-done.11, s32[2]{0:T(128)S(1)} %copy-done.12, s32[6]{0:T(128)S(1)} %reshape.28.orders, f32[1,128]{1,0:T(1,128)S(1)} %copy-done.13), custom_call_target="tpu_custom_call" | custom-call | flops 10240000 | bytes 819200 | tf_op jit(solution)/shard_map/tab/pallas_call | solution.py:464
  41.5 2.9 %kp.1 = (f32[288,128]{1,0:T(8,128)S(1)}, f32[288,128]{1,0:T(8,128)S(1)}, f32[288,128]{1,0:T(8,128)S(1)}, f32[288,128]{1,0:T(8,128)S(1)}, bf16[288,2048]{1,0:T(8,128)(2,1)S(1)}) custom-call(s32[2]{0:T(128)S(1)} %pad_add_fusion.pos, bf16[64,2048]{1,0:T(8,128)(2,1)S(1)} %get-tuple-element.43.refs_0_, bf16[64,2048]{1,0:T(8,128)(2,1)} %collective-permute-done.5.refs_1_, ...), custom_call_target="tpu_custom_call" | custom-call | flops 603979776 | bytes 3276800 | tf_op jit(solution)/shard_map/kp/pallas_call | solution.py:488
  44.4 2.6 %vp.1 = (f32[288,128]{1,0:T(8,128)S(1)}, bf16[288,128]{1,0:T(8,128)(2,1)S(1)}, bf16[288,128]{1,0:T(8,128)(2,1)S(1)}, bf16[288,128]{1,0:T(8,128)(2,1)S(1)}) custom-call(s32[2]{0:T(128)S(1)} %pad_add_fusion.pos, bf16[288,2048]{1,0:T(8,128)(2,1)S(1)} %get-tuple-element.32.rows_ref, bf16[512,512]{1,0:T(8,128)(2,1)S(1)} %copy-done.4, ...), custom_call_target="tpu_custom_call" | custom-call | flops 603979776 | bytes 3276800 | tf_op jit(solution)/shard_map/vp/pallas_call | solution.py:503
  47.0 4.7 %collective-permute-start.23 = (bf16[288,128]{1,0:T(8,128)(2,1)S(1)}, bf16[288,128]{1,0:T(8,128)(2,1)S(1)}, u32[]{:S(2)}, u32[]{:S(2)}) collective-permute-start(bf16[288,128]{1,0:T(8,128)(2,1)S(1)} %get-tuple-element.34), channel_id=1, source_target_pairs={{0,4},{1,5},{2,6},{3,7},{4,8},{5,9},{6,10},{7,11},{8,12},{9,13},{1... | collective-permute-start | bytes 221192 | tf_op jit(solution)/shard_map/ppermute | solution.py:411
  51.7 3.2 %collective-permute-start.24 = (bf16[288,128]{1,0:T(8,128)(2,1)S(1)}, bf16[288,128]{1,0:T(8,128)(2,1)S(1)}, u32[]{:S(2)}, u32[]{:S(2)}) collective-permute-start(bf16[288,128]{1,0:T(8,128)(2,1)S(1)} %get-tuple-element.35), channel_id=1, source_target_pairs={{0,8},{1,9},{2,10},{3,11},{4,12},{5,13},{6,14},{7,15},{8,0},{9,1},... | collective-permute-start | bytes 221192 | tf_op jit(solution)/shard_map/ppermute | solution.py:411
  55.0 2.1 %collective-permute-start.14 = (f16[288,128]{1,0:T(8,128)(2,1)S(1)}, f16[288,128]{1,0:T(8,128)(2,1)S(1)}, u32[]{:S(2)}, u32[]{:S(2)}) collective-permute-start(f16[288,128]{1,0:T(8,128)(2,1)S(1)} %convert_element_type.65), channel_id=1, source_target_pairs={{0,4},{1,5},{2,6},{3,7},{4,8},{5,9},{6,10},{7,11},{8,12},{9,13},{1... | collective-permute-start | bytes 221192 | tf_op jit(solution)/shard_map/ppermute | solution.py:411
  57.2 1.4 %add.83 = f32[2,4,256,128]{3,2,1,0:T(8,128)S(1)} add(f32[2,4,256,128]{3,2,1,0:T(8,128)S(1)} %get-tuple-element.22, f32[2,4,256,128]{3,2,1,0:T(8,128)} %collective-permute-done) | non-fusion elementwise | flops 262144 | bytes 3145728 | tf_op jit(solution)/shard_map/add | solution.py:452
  58.7 2.5 %collective-permute-start.16 = (f16[288,128]{1,0:T(8,128)(2,1)S(1)}, f16[288,128]{1,0:T(8,128)(2,1)S(1)}, u32[]{:S(2)}, u32[]{:S(2)}) collective-permute-start(f16[288,128]{1,0:T(8,128)(2,1)S(1)} %convert_element_type.69), channel_id=1, source_target_pairs={{0,12},{1,13},{2,14},{3,15},{4,0},{5,1},{6,2},{7,3},{8,4},{9,5},{1... | collective-permute-start | bytes 221192 | tf_op jit(solution)/shard_map/ppermute | solution.py:411
  61.1 1.8 %collective-permute-done.24 = bf16[288,128]{1,0:T(8,128)(2,1)S(1)} collective-permute-done((bf16[288,128]{1,0:T(8,128)(2,1)S(1)}, bf16[288,128]{1,0:T(8,128)(2,1)S(1)}, u32[]{:S(2)}, u32[]{:S(2)}) %collective-permute-start.24) | collective-permute-done | bytes 73760 | tf_op jit(solution)/shard_map/ppermute | solution.py:411
  63.4 1.7 %collective-permute-start.27 = (bf16[288,128]{1,0:T(8,128)(2,1)S(1)}, bf16[288,128]{1,0:T(8,128)(2,1)S(1)}, u32[]{:S(2)}, u32[]{:S(2)}) collective-permute-start(bf16[288,128]{1,0:T(8,128)(2,1)S(1)} %add_convert_fusion.refs_4_), channel_id=1, source_target_pairs={{0,2},{1,3},{2,0},{3,1},{4,6},{5,7},{6,4},{7,5},{8,10},{9,11},{10,... | collective-permute-start | bytes 221192 | tf_op jit(solution)/shard_map/ppermute | solution.py:397
  65.1 1.5 %collective-permute-done.15 = f16[288,128]{1,0:T(8,128)(2,1)S(1)} collective-permute-done((f16[288,128]{1,0:T(8,128)(2,1)S(1)}, f16[288,128]{1,0:T(8,128)(2,1)S(1)}, u32[]{:S(2)}, u32[]{:S(2)}) %collective-permute-start.15) | collective-permute-done | bytes 73760 | tf_op jit(solution)/shard_map/ppermute | solution.py:411
  67.2 2.7 %collective-permute-done.1 = f16[1,4,256,128]{3,2,1,0:T(8,128)(2,1)S(1)} collective-permute-done((f16[1,4,256,128]{3,2,1,0:T(8,128)(2,1)S(1)}, f16[1,4,256,128]{3,2,1,0:T(8,128)(2,1)S(1)}, u32[]{:S(2)}, u32[]{:S(2)}) %collective-permute-start.1) | collective-permute-done | bytes 262176 | tf_op jit(solution)/shard_map/ppermute | solution.py:397
  71.3 2.7 %collective-permute-start.4 = (f16[256,128]{1,0:T(8,128)(2,1)S(1)}, f16[256,128]{1,0:T(8,128)(2,1)S(1)}, u32[]{:S(2)}, u32[]{:S(2)}) collective-permute-start(f16[256,128]{1,0:T(8,128)(2,1)S(1)} %get-tuple-element.46), channel_id=1, source_target_pairs={{0,12},{1,13},{2,14},{3,15},{4,0},{5,1},{6,2},{7,3},{8,4},{9,5},{1... | collective-permute-start | bytes 196616 | tf_op jit(solution)/shard_map/ppermute | solution.py:411
  74.9 1.3 %collective-permute-done.2 = f16[256,128]{1,0:T(8,128)(2,1)S(1)} collective-permute-done((f16[256,128]{1,0:T(8,128)(2,1)S(1)}, f16[256,128]{1,0:T(8,128)(2,1)S(1)}, u32[]{:S(2)}, u32[]{:S(2)}) %collective-permute-start.2) | collective-permute-done | bytes 65568 | tf_op jit(solution)/shard_map/ppermute | solution.py:411
  77.8 2.5 %attend.1.refs_0_ = bf16[256,128]{1,0:T(8,128)(2,1)S(1)} custom-call(s32[2]{0:T(128)S(1)} %pad_add_fusion.pos, f32[256,128]{1,0:T(8,128)S(1)} %fusion.2.q_ref, f32[128,128]{1,0:T(8,128)S(1)} %get-tuple-element.24.cos_ref, f32[128,128]{1,0:T(8,128)S(1)} %get-tuple-element.25.sin_ref, bf16[800,128]{1,0:T(8,128)(2,1)S(1)} %turn.1.refs_0_, ...), custom_call_target="tpu_custom_call" | custom-call | tf_op jit(solution)/shard_map/attend/pallas_call | solution.py:541
  81.5 2.7 %collective-permute-start.33 = (bf16[256,128]{1,0:T(8,128)(2,1)S(1)}, bf16[256,128]{1,0:T(8,128)(2,1)S(1)}, u32[]{:S(2)}, u32[]{:S(2)}) collective-permute-start(bf16[256,128]{1,0:T(8,128)(2,1)S(1)} %attend.1.refs_0_), channel_id=1, source_target_pairs={{0,12},{1,13},{2,14},{3,15},{4,0},{5,1},{6,2},{7,3},{8,4},{9,5},{1... | collective-permute-start | bytes 196616 | tf_op jit(solution)/shard_map/ppermute | solution.py:411
  84.2 1.8 %collective-permute-start.39 = (bf16[256,128]{1,0:T(8,128)(2,1)S(1)}, bf16[256,128]{1,0:T(8,128)(2,1)S(1)}, u32[]{:S(2)}, u32[]{:S(2)}) collective-permute-start(bf16[256,128]{1,0:T(8,128)(2,1)S(1)} %attend.1.refs_0_), channel_id=1, source_target_pairs={{0,2},{1,3},{2,0},{3,1},{4,6},{5,7},{6,4},{7,5},{8,10},{9,11},{10,... | collective-permute-start | bytes 196616 | tf_op jit(solution)/shard_map/ppermute | solution.py:397
  88.4 1.8 %collective-permute-start.31 = (bf16[256,128]{1,0:T(8,128)(2,1)S(1)}, bf16[256,128]{1,0:T(8,128)(2,1)S(1)}, u32[]{:S(2)}, u32[]{:S(2)}) collective-permute-start(bf16[256,128]{1,0:T(8,128)(2,1)S(1)} %collective-permute-done.30.refs_1_), channel_id=1, source_target_pairs={{0,2},{1,3},{2,0},{3,1},{4,6},{5,7},{6,4},{7,5},{8,10},{9,11},{10,... | collective-permute-start | bytes 196616 | tf_op jit(solution)/shard_map/ppermute | solution.py:397
  91.7 1.4 %collective-permute-start.34 = (bf16[256,128]{1,0:T(8,128)(2,1)S(1)}, bf16[256,128]{1,0:T(8,128)(2,1)S(1)}, u32[]{:S(2)}, u32[]{:S(2)}) collective-permute-start(bf16[256,128]{1,0:T(8,128)(2,1)S(1)} %collective-permute-done.33.refs_2_), channel_id=1, source_target_pairs={{0,2},{1,3},{2,0},{3,1},{4,6},{5,7},{6,4},{7,5},{8,10},{9,11},{10,... | collective-permute-start | bytes 196616 | tf_op jit(solution)/shard_map/ppermute | solution.py:397
  93.7 1.6 %collective-permute-done.32.refs_2_ = bf16[256,128]{1,0:T(8,128)(2,1)S(1)} collective-permute-done((bf16[256,128]{1,0:T(8,128)(2,1)S(1)}, bf16[256,128]{1,0:T(8,128)(2,1)S(1)}, u32[]{:S(2)}, u32[]{:S(2)}) %collective-permute-start.32) | collective-permute-done | bytes 65568 | tf_op jit(solution)/shard_map/ppermute | solution.py:397
  99.7 1.3 %collective-permute-start.45 = (f32[8,128]{1,0:T(8,128)S(1)}, f32[8,128]{1,0:T(8,128)S(1)}, u32[]{:S(2)}, u32[]{:S(2)}) collective-permute-start(f32[8,128]{1,0:T(8,128)S(1)} %add.101), channel_id=1, source_target_pairs={{0,2},{1,3},{2,0},{3,1},{4,6},{5,7},{6,4},{7,5},{8,10},{9,11},{10,... | collective-permute-start | bytes 12296 | tf_op jit(solution)/shard_map/ppermute | solution.py:397
  101.0 2.3 %collective-permute-done.45 = f32[8,128]{1,0:T(8,128)S(1)} collective-permute-done((f32[8,128]{1,0:T(8,128)S(1)}, f32[8,128]{1,0:T(8,128)S(1)}, u32[]{:S(2)}, u32[]{:S(2)}) %collective-permute-start.45) | collective-permute-done | bytes 4128 | tf_op jit(solution)/shard_map/ppermute | solution.py:397
  103.3 3.6 %collective-permute-done.46 = f32[8,128]{1,0:T(8,128)S(1)} collective-permute-done((f32[8,128]{1,0:T(8,128)S(1)}, f32[8,128]{1,0:T(8,128)S(1)}, u32[]{:S(2)}, u32[]{:S(2)}) %collective-permute-start.46) | collective-permute-done | bytes 4128 | tf_op jit(solution)/shard_map/ppermute | solution.py:397
  107.8 3.6 %collective-permute-done.47 = f32[8,128]{1,0:T(8,128)S(1)} collective-permute-done((f32[8,128]{1,0:T(8,128)S(1)}, f32[8,128]{1,0:T(8,128)S(1)}, u32[]{:S(2)}, u32[]{:S(2)}) %collective-permute-start.47) | collective-permute-done | bytes 4128 | tf_op jit(solution)/shard_map/ppermute | solution.py:397
  (128 shorter events, 26.5 us)
Async XLA Ops:
  0.0 15.0 %collective-permute-start.9 = (bf16[128,512]{1,0:T(8,128)(2,1)}, bf16[128,512]{1,0:T(8,128)(2,1)}, u32[]{:S(2)}, u32[]{:S(2)}) collective-permute-start(bf16[128,512]{1,0:T(8,128)(2,1)} %refs_4_.1), channel_id=1, source_target_pairs={{0,2},{1,3},{2,0},{3,1},{4,6},{5,7},{6,4},{7,5},{8,10},{9,11},{10,... | collective-permute-start | bytes 393224 | tf_op jit(solution)/shard_map/ppermute | solution.py:397
  3.1 12.0 %collective-permute-start.8 = (bf16[128,512]{1,0:T(8,128)(2,1)}, bf16[128,512]{1,0:T(8,128)(2,1)}, u32[]{:S(2)}, u32[]{:S(2)}) collective-permute-start(bf16[128,512]{1,0:T(8,128)(2,1)} %refs_4_.1), channel_id=1, source_target_pairs={{0,1},{1,0},{2,3},{3,2},{4,5},{5,4},{6,7},{7,6},{8,9},{9,8},{10,11... | collective-permute-start | bytes 393224 | tf_op jit(solution)/shard_map/ppermute | solution.py:397
  5.2 12.6 %collective-permute-start.5 = (bf16[64,2048]{1,0:T(8,128)(2,1)}, bf16[64,2048]{1,0:T(8,128)(2,1)}, u32[]{:S(2)}, u32[]{:S(2)}) collective-permute-start(bf16[64,2048]{1,0:T(8,128)(2,1)} %get-tuple-element.42), channel_id=1, source_target_pairs={{0,4},{1,5},{2,6},{3,7},{4,8},{5,9},{6,10},{7,11},{8,12},{9,13},{1... | collective-permute-start | bytes 786440 | tf_op jit(solution)/shard_map/ppermute | solution.py:411
  6.7 26.1 %collective-permute-start.12 = (bf16[512,512]{1,0:T(8,128)(2,1)}, bf16[512,512]{1,0:T(8,128)(2,1)S(1)}, u32[]{:S(2)}, u32[]{:S(2)}) collective-permute-start(bf16[512,512]{1,0:T(8,128)(2,1)} %refs_8_.3), channel_id=1, source_target_pairs={{0,2},{1,3},{2,0},{3,1},{4,6},{5,7},{6,4},{7,5},{8,10},{9,11},{10,... | collective-permute-start | bytes 1572872 | tf_op jit(solution)/shard_map/ppermute | solution.py:397
  7.3 26.7 %collective-permute-start.21 = (bf16[512,512]{1,0:T(8,128)(2,1)}, bf16[512,512]{1,0:T(8,128)(2,1)S(1)}, u32[]{:S(2)}, u32[]{:S(2)}) collective-permute-start(bf16[512,512]{1,0:T(8,128)(2,1)} %refs_0_.1), channel_id=1, source_target_pairs={{0,2},{1,3},{2,0},{3,1},{4,6},{5,7},{6,4},{7,5},{8,10},{9,11},{10,... | collective-permute-start | bytes 1572872 | tf_op jit(solution)/shard_map/ppermute | solution.py:397
  15.0 42.0 %collective-permute-start = (f32[2,4,256,128]{3,2,1,0:T(8,128)}, f32[2,4,256,128]{3,2,1,0:T(8,128)}, u32[]{:S(2)}, u32[]{:S(2)}) collective-permute-start(f32[2,4,256,128]{3,2,1,0:T(8,128)} %get-tuple-element.23), channel_id=1, source_target_pairs={{0,1},{1,0},{2,3},{3,2},{4,5},{5,4},{6,7},{7,6},{8,9},{9,8},{10,11... | collective-permute-start | bytes 3145736 | tf_op jit(solution)/shard_map/ppermute | solution.py:397
  15.1 15.8 %collective-permute-start.6 = (bf16[64,2048]{1,0:T(8,128)(2,1)S(1)}, bf16[64,2048]{1,0:T(8,128)(2,1)S(1)}, u32[]{:S(2)}, u32[]{:S(2)}) collective-permute-start(bf16[64,2048]{1,0:T(8,128)(2,1)S(1)} %copy-done.15), channel_id=1, source_target_pairs={{0,8},{1,9},{2,10},{3,11},{4,12},{5,13},{6,14},{7,15},{8,0},{9,1},... | collective-permute-start | bytes 786440 | tf_op jit(solution)/shard_map/ppermute | solution.py:411
  17.7 13.9 %collective-permute-start.7 = (bf16[64,2048]{1,0:T(8,128)(2,1)S(1)}, bf16[64,2048]{1,0:T(8,128)(2,1)S(1)}, u32[]{:S(2)}, u32[]{:S(2)}) collective-permute-start(bf16[64,2048]{1,0:T(8,128)(2,1)S(1)} %copy-done.14), channel_id=1, source_target_pairs={{0,12},{1,13},{2,14},{3,15},{4,0},{5,1},{6,2},{7,3},{8,4},{9,5},{1... | collective-permute-start | bytes 786440 | tf_op jit(solution)/shard_map/ppermute | solution.py:411
  32.3 6.4 %collective-permute-start.11 = (bf16[512,512]{1,0:T(8,128)(2,1)S(1)}, bf16[512,512]{1,0:T(8,128)(2,1)}, u32[]{:S(2)}, u32[]{:S(2)}) collective-permute-start(bf16[512,512]{1,0:T(8,128)(2,1)S(1)} %copy-done.3), channel_id=1, source_target_pairs={{0,1},{1,0},{2,3},{3,2},{4,5},{5,4},{6,7},{7,6},{8,9},{9,8},{10,11... | collective-permute-start | bytes 1572872 | tf_op jit(solution)/shard_map/ppermute | solution.py:397
  32.8 5.9 %collective-permute-start.13 = (bf16[512,512]{1,0:T(8,128)(2,1)S(1)}, bf16[512,512]{1,0:T(8,128)(2,1)}, u32[]{:S(2)}, u32[]{:S(2)}) collective-permute-start(bf16[512,512]{1,0:T(8,128)(2,1)S(1)} %collective-permute-done.12.refs_10_), channel_id=1, source_target_pairs={{0,1},{1,0},{2,3},{3,2},{4,5},{5,4},{6,7},{7,6},{8,9},{9,8},{10,11... | collective-permute-start | bytes 1572872 | tf_op jit(solution)/shard_map/ppermute | solution.py:397
  33.8 10.6 %collective-permute-start.20 = (bf16[512,512]{1,0:T(8,128)(2,1)S(1)}, bf16[512,512]{1,0:T(8,128)(2,1)}, u32[]{:S(2)}, u32[]{:S(2)}) collective-permute-start(bf16[512,512]{1,0:T(8,128)(2,1)S(1)} %copy-done.4), channel_id=1, source_target_pairs={{0,1},{1,0},{2,3},{3,2},{4,5},{5,4},{6,7},{7,6},{8,9},{9,8},{10,11... | collective-permute-start | bytes 1572872 | tf_op jit(solution)/shard_map/ppermute | solution.py:397
  34.0 10.4 %collective-permute-start.22 = (bf16[512,512]{1,0:T(8,128)(2,1)S(1)}, bf16[512,512]{1,0:T(8,128)(2,1)}, u32[]{:S(2)}, u32[]{:S(2)}) collective-permute-start(bf16[512,512]{1,0:T(8,128)(2,1)S(1)} %collective-permute-done.21.refs_2_), channel_id=1, source_target_pairs={{0,1},{1,0},{2,3},{3,2},{4,5},{5,4},{6,7},{7,6},{8,9},{9,8},{10,11... | collective-permute-start | bytes 1572872 | tf_op jit(solution)/shard_map/ppermute | solution.py:397
  47.0 11.6 %collective-permute-start.23 = (bf16[288,128]{1,0:T(8,128)(2,1)S(1)}, bf16[288,128]{1,0:T(8,128)(2,1)S(1)}, u32[]{:S(2)}, u32[]{:S(2)}) collective-permute-start(bf16[288,128]{1,0:T(8,128)(2,1)S(1)} %get-tuple-element.34), channel_id=1, source_target_pairs={{0,4},{1,5},{2,6},{3,7},{4,8},{5,9},{6,10},{7,11},{8,12},{9,13},{1... | collective-permute-start | bytes 221192 | tf_op jit(solution)/shard_map/ppermute | solution.py:411
  51.7 11.2 %collective-permute-start.24 = (bf16[288,128]{1,0:T(8,128)(2,1)S(1)}, bf16[288,128]{1,0:T(8,128)(2,1)S(1)}, u32[]{:S(2)}, u32[]{:S(2)}) collective-permute-start(bf16[288,128]{1,0:T(8,128)(2,1)S(1)} %get-tuple-element.35), channel_id=1, source_target_pairs={{0,8},{1,9},{2,10},{3,11},{4,12},{5,13},{6,14},{7,15},{8,0},{9,1},... | collective-permute-start | bytes 221192 | tf_op jit(solution)/shard_map/ppermute | solution.py:411
  55.0 8.3 %collective-permute-start.25 = (bf16[288,128]{1,0:T(8,128)(2,1)S(1)}, bf16[288,128]{1,0:T(8,128)(2,1)S(1)}, u32[]{:S(2)}, u32[]{:S(2)}) collective-permute-start(bf16[288,128]{1,0:T(8,128)(2,1)S(1)} %get-tuple-element.36), channel_id=1, source_target_pairs={{0,12},{1,13},{2,14},{3,15},{4,0},{5,1},{6,2},{7,3},{8,4},{9,5},{1... | collective-permute-start | bytes 221192 | tf_op jit(solution)/shard_map/ppermute | solution.py:411
  55.0 10.1 %collective-permute-start.14 = (f16[288,128]{1,0:T(8,128)(2,1)S(1)}, f16[288,128]{1,0:T(8,128)(2,1)S(1)}, u32[]{:S(2)}, u32[]{:S(2)}) collective-permute-start(f16[288,128]{1,0:T(8,128)(2,1)S(1)} %convert_element_type.65), channel_id=1, source_target_pairs={{0,4},{1,5},{2,6},{3,7},{4,8},{5,9},{6,10},{7,11},{8,12},{9,13},{1... | collective-permute-start | bytes 221192 | tf_op jit(solution)/shard_map/ppermute | solution.py:411
  57.1 9.5 %collective-permute-start.15 = (f16[288,128]{1,0:T(8,128)(2,1)S(1)}, f16[288,128]{1,0:T(8,128)(2,1)S(1)}, u32[]{:S(2)}, u32[]{:S(2)}) collective-permute-start(f16[288,128]{1,0:T(8,128)(2,1)S(1)} %convert_element_type.67), channel_id=1, source_target_pairs={{0,8},{1,9},{2,10},{3,11},{4,12},{5,13},{6,14},{7,15},{8,0},{9,1},... | collective-permute-start | bytes 221192 | tf_op jit(solution)/shard_map/ppermute | solution.py:411
  58.7 7.9 %collective-permute-start.16 = (f16[288,128]{1,0:T(8,128)(2,1)S(1)}, f16[288,128]{1,0:T(8,128)(2,1)S(1)}, u32[]{:S(2)}, u32[]{:S(2)}) collective-permute-start(f16[288,128]{1,0:T(8,128)(2,1)S(1)} %convert_element_type.69), channel_id=1, source_target_pairs={{0,12},{1,13},{2,14},{3,15},{4,0},{5,1},{6,2},{7,3},{8,4},{9,5},{1... | collective-permute-start | bytes 221192 | tf_op jit(solution)/shard_map/ppermute | solution.py:411
  63.0 7.0 %collective-permute-start.1 = (f16[1,4,256,128]{3,2,1,0:T(8,128)(2,1)S(1)}, f16[1,4,256,128]{3,2,1,0:T(8,128)(2,1)S(1)}, u32[]{:S(2)}, u32[]{:S(2)}) collective-permute-start(f16[1,4,256,128]{3,2,1,0:T(8,128)(2,1)S(1)} %slice_convert_fusion), channel_id=1, source_target_pairs={{0,2},{1,3},{2,0},{3,1},{4,6},{5,7},{6,4},{7,5},{8,10},{9,11},{10,... | collective-permute-start | bytes 786440 | tf_op jit(solution)/shard_map/ppermute | solution.py:397
  63.4 10.6 %collective-permute-start.27 = (bf16[288,128]{1,0:T(8,128)(2,1)S(1)}, bf16[288,128]{1,0:T(8,128)(2,1)S(1)}, u32[]{:S(2)}, u32[]{:S(2)}) collective-permute-start(bf16[288,128]{1,0:T(8,128)(2,1)S(1)} %add_convert_fusion.refs_4_), channel_id=1, source_target_pairs={{0,2},{1,3},{2,0},{3,1},{4,6},{5,7},{6,4},{7,5},{8,10},{9,11},{10,... | collective-permute-start | bytes 221192 | tf_op jit(solution)/shard_map/ppermute | solution.py:397
  66.8 8.1 %collective-permute-start.18 = (bf16[800,128]{1,0:T(8,128)(2,1)S(1)}, bf16[800,128]{1,0:T(8,128)(2,1)S(1)}, u32[]{:S(2)}, u32[]{:S(2)}) collective-permute-start(bf16[800,128]{1,0:T(8,128)(2,1)S(1)} %turn.1.refs_0_), channel_id=1, source_target_pairs={{0,2},{1,3},{2,0},{3,1},{4,6},{5,7},{6,4},{7,5},{8,10},{9,11},{10,... | collective-permute-start | bytes 614408 | tf_op jit(solution)/shard_map/ppermute | solution.py:397
  70.1 6.1 %collective-permute-start.2 = (f16[256,128]{1,0:T(8,128)(2,1)S(1)}, f16[256,128]{1,0:T(8,128)(2,1)S(1)}, u32[]{:S(2)}, u32[]{:S(2)}) collective-permute-start(f16[256,128]{1,0:T(8,128)(2,1)S(1)} %get-tuple-element.45), channel_id=1, source_target_pairs={{0,4},{1,5},{2,6},{3,7},{4,8},{5,9},{6,10},{7,11},{8,12},{9,13},{1... | collective-permute-start | bytes 196616 | tf_op jit(solution)/shard_map/ppermute | solution.py:411
  70.2 6.1 %collective-permute-start.3 = (f16[256,128]{1,0:T(8,128)(2,1)S(1)}, f16[256,128]{1,0:T(8,128)(2,1)S(1)}, u32[]{:S(2)}, u32[]{:S(2)}) collective-permute-start(f16[256,128]{1,0:T(8,128)(2,1)S(1)} %get-tuple-element.47), channel_id=1, source_target_pairs={{0,8},{1,9},{2,10},{3,11},{4,12},{5,13},{6,14},{7,15},{8,0},{9,1},... | collective-permute-start | bytes 196616 | tf_op jit(solution)/shard_map/ppermute | solution.py:411
  71.3 5.6 %collective-permute-start.4 = (f16[256,128]{1,0:T(8,128)(2,1)S(1)}, f16[256,128]{1,0:T(8,128)(2,1)S(1)}, u32[]{:S(2)}, u32[]{:S(2)}) collective-permute-start(f16[256,128]{1,0:T(8,128)(2,1)S(1)} %get-tuple-element.46), channel_id=1, source_target_pairs={{0,12},{1,13},{2,14},{3,15},{4,0},{5,1},{6,2},{7,3},{8,4},{9,5},{1... | collective-permute-start | bytes 196616 | tf_op jit(solution)/shard_map/ppermute | solution.py:411
  80.3 6.8 %collective-permute-start.30 = (bf16[256,128]{1,0:T(8,128)(2,1)S(1)}, bf16[256,128]{1,0:T(8,128)(2,1)S(1)}, u32[]{:S(2)}, u32[]{:S(2)}) collective-permute-start(bf16[256,128]{1,0:T(8,128)(2,1)S(1)} %attend.1.refs_0_), channel_id=1, source_target_pairs={{0,4},{1,5},{2,6},{3,7},{4,8},{5,9},{6,10},{7,11},{8,12},{9,13},{1... | collective-permute-start | bytes 196616 | tf_op jit(solution)/shard_map/ppermute | solution.py:411
  81.5 5.7 %collective-permute-start.33 = (bf16[256,128]{1,0:T(8,128)(2,1)S(1)}, bf16[256,128]{1,0:T(8,128)(2,1)S(1)}, u32[]{:S(2)}, u32[]{:S(2)}) collective-permute-start(bf16[256,128]{1,0:T(8,128)(2,1)S(1)} %attend.1.refs_0_), channel_id=1, source_target_pairs={{0,12},{1,13},{2,14},{3,15},{4,0},{5,1},{6,2},{7,3},{8,4},{9,5},{1... | collective-permute-start | bytes 196616 | tf_op jit(solution)/shard_map/ppermute | solution.py:411
  86.0 5.2 %collective-permute-start.29 = (bf16[256,128]{1,0:T(8,128)(2,1)S(1)}, bf16[256,128]{1,0:T(8,128)(2,1)S(1)}, u32[]{:S(2)}, u32[]{:S(2)}) collective-permute-start(bf16[256,128]{1,0:T(8,128)(2,1)S(1)} %attend.1.refs_0_), channel_id=1, source_target_pairs={{0,8},{1,9},{2,10},{3,11},{4,12},{5,13},{6,14},{7,15},{8,0},{9,1},... | collective-permute-start | bytes 196616 | tf_op jit(solution)/shard_map/ppermute | solution.py:411
  86.0 5.8 %collective-permute-start.40 = (bf16[256,128]{1,0:T(8,128)(2,1)S(1)}, bf16[256,128]{1,0:T(8,128)(2,1)S(1)}, u32[]{:S(2)}, u32[]{:S(2)}) collective-permute-start(bf16[256,128]{1,0:T(8,128)(2,1)S(1)} %attend.1.refs_0_), channel_id=1, source_target_pairs={{0,1},{1,0},{2,3},{3,2},{4,5},{5,4},{6,7},{7,6},{8,9},{9,8},{10,11... | collective-permute-start | bytes 196616 | tf_op jit(solution)/shard_map/ppermute | solution.py:397
  87.1 6.0 %collective-permute-start.41 = (bf16[256,128]{1,0:T(8,128)(2,1)S(1)}, bf16[256,128]{1,0:T(8,128)(2,1)S(1)}, u32[]{:S(2)}, u32[]{:S(2)}) collective-permute-start(bf16[256,128]{1,0:T(8,128)(2,1)S(1)} %collective-permute-done.30.refs_1_), channel_id=1, source_target_pairs={{0,1},{1,0},{2,3},{3,2},{4,5},{5,4},{6,7},{7,6},{8,9},{9,8},{10,11... | collective-permute-start | bytes 196616 | tf_op jit(solution)/shard_map/ppermute | solution.py:397
  87.1 6.0 %collective-permute-start.42 = (bf16[256,128]{1,0:T(8,128)(2,1)S(1)}, bf16[256,128]{1,0:T(8,128)(2,1)S(1)}, u32[]{:S(2)}, u32[]{:S(2)}) collective-permute-start(bf16[256,128]{1,0:T(8,128)(2,1)S(1)} %collective-permute-done.33.refs_2_), channel_id=1, source_target_pairs={{0,1},{1,0},{2,3},{3,2},{4,5},{5,4},{6,7},{7,6},{8,9},{9,8},{10,11... | collective-permute-start | bytes 196616 | tf_op jit(solution)/shard_map/ppermute | solution.py:397
  88.4 5.2 %collective-permute-start.31 = (bf16[256,128]{1,0:T(8,128)(2,1)S(1)}, bf16[256,128]{1,0:T(8,128)(2,1)S(1)}, u32[]{:S(2)}, u32[]{:S(2)}) collective-permute-start(bf16[256,128]{1,0:T(8,128)(2,1)S(1)} %collective-permute-done.30.refs_1_), channel_id=1, source_target_pairs={{0,2},{1,3},{2,0},{3,1},{4,6},{5,7},{6,4},{7,5},{8,10},{9,11},{10,... | collective-permute-start | bytes 196616 | tf_op jit(solution)/shard_map/ppermute | solution.py:397
  106.9 4.5 %collective-permute-start.47 = (f32[8,128]{1,0:T(8,128)S(1)}, f32[8,128]{1,0:T(8,128)S(1)}, u32[]{:S(2)}, u32[]{:S(2)}) collective-permute-start(f32[8,128]{1,0:T(8,128)S(1)} %add.103), channel_id=1, source_target_pairs={{0,8},{1,9},{2,10},{3,11},{4,12},{5,13},{6,14},{7,15},{8,0},{9,1},... | collective-permute-start | bytes 12296 | tf_op jit(solution)/shard_map/ppermute | solution.py:397
  (34 other events, 343.5 us)
